TPU v7x, 128 devices: a whole 4x4x4 slice. The times are simulated.
128 devices in a mesh: wall: 32 (over y, x, core), surf: 4 (over z).
Axes of the slice: x: 4, y: 4, z: 4, core: 2. Of those that a mesh axis runs over, the one named last changes fastest.
Arguments:
- state: bfloat16 [8192, 162], P(('wall', 'surf')), may hold values from -6 to 6
- source: bfloat16 [8192, 162], P(('wall', 'surf')), may hold values from -6 to 6
- face_coef: float32 [8192, 4], P(('wall', 'surf')), may hold values from 0.1 to 0.5
- neighbour: int32 [8192, 4], P(('wall', 'surf')), may hold values from 0 to 191
- lift: bfloat16 [162, 162], replicated, may hold values from -0.5 to 0.5
- elem_slot: int32 [64, 128], P('wall', 'surf'), may hold values from 0 to 63, as said below
- line_len: int32 [128], P('surf'), may hold values from 32 to 64
- dinv: bfloat16 [64, 128, 162, 162], P('wall', 'surf'), may hold values from -0.3 to 1.2
- lower: bfloat16 [64, 128, 162, 162], P('wall', 'surf'), may hold values from -1.4 to 0.4
- upper: bfloat16 [64, 128, 162, 162], P('wall', 'surf'), may hold values from -0.4 to 1.4
Outputs:
- solution: float32 [64, 128, 162], P('wall', 'surf')
Inputs may be any that keep to these rules, and one draw needn't show every extreme that they name: `elem_slot`: on each device the entries form a permutation of its 64 slots.
All inputs are finite; a program needn't handle non-finite values.
Results may differ from a plain program's by a relative error of at most 0.0023.
Values may be sent and summed in bfloat16 or wider, within the bound.
A program may use at most 128 MiB of HBM per device.

v0:
```python
import jax
import jax.numpy as jnp
from jax import lax
from jax.sharding import PartitionSpec as P


def padded(cells, sides, width):
    for axis, dim in sides:
        count = lax.axis_size(axis)
        head = lax.slice_in_dim(cells, 0, width, axis=dim)
        tail = lax.slice_in_dim(cells, cells.shape[dim] - width, cells.shape[dim], axis=dim)
        cells = jnp.concatenate(
            [
                lax.ppermute(tail, axis, [(i, (i + 1) % count) for i in range(count)]),
                cells,
                lax.ppermute(head, axis, [((i + 1) % count, i) for i in range(count)]),
            ],
            axis=dim,
        )
    return cells


def passed_along(block, axis, distance):
    devices = range(lax.axis_size(axis))
    route = [(i - distance, i) for i in devices if i - distance in devices]
    return lax.ppermute(block, axis, route)


def apply_block(matrix, vector):
    return jnp.einsum(
        "lij,lj->li", matrix.astype(jnp.float32), vector, precision=lax.Precision.HIGHEST
    )


def forward_step(carried, items):
    dblock, lblock, rhs_now, act_now = items
    value = act_now[:, None] * apply_block(dblock, rhs_now - apply_block(lblock, carried))
    return (value, value)


def backward_step(carried, items):
    dblock, ublock, y_now, act_now = items
    value = act_now[:, None] * (y_now - apply_block(dblock, apply_block(ublock, carried)))
    return (value, value)


def per_device(state, source, face_coef, neighbour, lift, elem_slot, line_len, dinv, lower, upper):
    slots = state.shape[0]
    extended = padded(state, (("surf", 0),), slots)
    nb_vals = jnp.take(extended, neighbour, axis=0).astype(jnp.float32)
    face_sum = jnp.sum(
        face_coef[:, :, None] * (state.astype(jnp.float32)[:, None, :] - nb_vals), axis=1
    ).astype(jnp.bfloat16)
    residual = source.astype(jnp.float32) - jnp.dot(
        face_sum, lift, preferred_element_type=jnp.float32
    )
    line_rhs = jnp.take(residual, elem_slot, axis=0)
    depth = dinv.shape[0]
    line_count = dinv.shape[1]
    width = dinv.shape[2]
    wall_index = lax.axis_index("wall")
    wall_count = lax.axis_size("wall")
    position = wall_index * depth + jnp.arange(depth, dtype=jnp.int32)
    active = (position[:, None] < line_len[None, :]).astype(jnp.float32)
    zeros_vec = jnp.zeros((line_count, width), jnp.float32)
    zero_vals = jnp.zeros((depth, line_count, width), jnp.float32)
    fwd_items = (dinv, lower, line_rhs, active)

    def fwd_compute(inputs):
        last, values = lax.scan(forward_step, inputs[0], fwd_items)
        return (values, last)

    def fwd_pass(inputs):
        return (inputs[1], jnp.zeros_like(inputs[0]))

    def fwd_hop(hop_index, carry):
        incoming, forward_vals = carry
        forward_vals, outgoing = lax.cond(
            wall_index == hop_index, fwd_compute, fwd_pass, (incoming, forward_vals)
        )
        received = passed_along(outgoing, "wall", 1)
        incoming = jnp.where(wall_index == hop_index + 1, received, incoming)
        return (incoming, forward_vals)

    incoming, forward_vals = lax.fori_loop(0, wall_count - 1, fwd_hop, (zeros_vec, zero_vals))
    forward_vals = lax.cond(
        wall_index == wall_count - 1,
        lambda inputs: fwd_compute(inputs)[0],
        lambda inputs: inputs[1],
        (incoming, forward_vals),
    )
    bwd_items = (dinv, upper, forward_vals, active)

    def bwd_compute(inputs):
        last, values = lax.scan(backward_step, inputs[0], bwd_items, reverse=True)
        return (values, last)

    def bwd_pass(inputs):
        return (inputs[1], jnp.zeros_like(inputs[0]))

    def bwd_hop(hop_index, carry):
        incoming, solution_vals = carry
        sender = wall_count - 1 - hop_index
        solution_vals, outgoing = lax.cond(
            wall_index == sender, bwd_compute, bwd_pass, (incoming, solution_vals)
        )
        received = passed_along(outgoing, "wall", -1)
        incoming = jnp.where(wall_index == sender - 1, received, incoming)
        return (incoming, solution_vals)

    incoming, solution_vals = lax.fori_loop(0, wall_count - 1, bwd_hop, (zeros_vec, zero_vals))
    solution = lax.cond(
        wall_index == 0,
        lambda inputs: bwd_compute(inputs)[0],
        lambda inputs: inputs[1],
        (incoming, solution_vals),
    )
    return solution


def solution(mesh):
    in_specs = (
        P(("wall", "surf"), None),
        P(("wall", "surf"), None),
        P(("wall", "surf"), None),
        P(("wall", "surf"), None),
        P(),
        P("wall", "surf"),
        P("surf"),
        P("wall", "surf", None, None),
        P("wall", "surf", None, None),
        P("wall", "surf", None, None),
    )
    out_specs = P("wall", "surf", None)
    return jax.shard_map(
        per_device, mesh=mesh, in_specs=in_specs, out_specs=out_specs, check_vma=False
    )
```

profile of v0, /device:TPU:1, one launch (start us, length us, event | category | flops | bytes accessed | tf_op | source)
XLA Modules:
  0.0 1445.2 jit_solution(9535877171591091339)
XLA Ops:
  9.2 7.9 copy.26
  17.4 7.9 copy.27
  25.3 8.0 copy.31
  36.4 414.1 %while.104 = (s32[]{:T(128)}, f32[32,162]{1,0:T(8,128)S(1)}, f32[2,32,162]{2,1,0:T(8,128)}, s32[]{:T(128)}, bf16[2,32,162,162]{3,2,1,0:T(8,128)(2,1)}, /*index=5...) while((s32[]{:T(128)}, f32[32,162]{1,0:T(8,128)S(1)}, ...), condition=%wide.region_6.7_spmd.clone, body=%wide.region_1.6_spmd.clone.sunk | while | flops 20181444 | bytes 5955229 | solution.py:85
  40.4 16.5 %collective-permute-done.1 = f32[32,162]{1,0:T(8,128)S(1)} collective-permute-done((f32[32,162]{1,0:T(8,128)S(1)}, f32[32,162]{1,0:T(8,128)S(1)}, u32[]{:S(2)}, u32[]{:S(2)}) %collective-permute-start.1) | collective-permute-done | bytes 20768 | tf_op jit(solution)/shard_map/while/body/eval_jaxpr/ppermute | solution.py:26
  57.0 17.5 %conditional.10 = (f32[2,32,162]{2,1,0:T(8,128)}, f32[32,162]{1,0:T(8,128)S(1)}) conditional(s32[]{:T(128)} %convert_element_type.78, f32[2,32,162]{2,1,0:T(8,128)} %get-tuple-element.1513, (f32[2,32]{1,0:T(2,128)S(1)}, bf16[2,32,162,162]{3,2,1,0:T(8,128)(2,1)}, f32[2,32,162]{2,1,0:T(8,128)S(1)}, bf16[2,32,162,162]{3,2,1,0:T(8,128)(2,1)}, ...), branch_computations={%region_2.2_spmd, %region_3.5_spmd} | conditional | flops 20165760 | bytes 5767989 | solution.py:78
  57.0 17.5 %while.100 = (s32[]{:T(128)}, f32[32,162]{1,0:T(8,128)S(1)}, f32[2,32,162]{2,1,0:T(8,128)}, f32[2,32]{1,0:T(2,128)S(1)}, bf16[2,32,162,162]{3,2,1,0:T(8,128)(2,1...) while((s32[]{:T(128)}, f32[32,162]{1,0:T(8,128)S(1)}, ...), condition=%wide.region_5.4_spmd, body=%wide.region_4.3_spmd.sunk | while | flops 20165760 | bytes 5726429 | solution.py:70
  77.7 21.6 %collective-permute-start.1 = (f32[32,162]{1,0:T(8,128)S(1)}, f32[32,162]{1,0:T(8,128)S(1)}, u32[]{:S(2)}, u32[]{:S(2)}) collective-permute-start(f32[32,162]{1,0:T(8,128)S(1)} %get-tuple-element.1343), channel_id=1, source_target_pairs={{0,4},{4,8},{8,12},{12,16},{16,20},{20,24},{24,28},{28,32},{32,36}... | collective-permute-start | bytes 62216 | tf_op jit(solution)/shard_map/while/body/eval_jaxpr/ppermute | solution.py:26
  105.7 17.1 %collective-permute-start.1 = (f32[32,162]{1,0:T(8,128)S(1)}, f32[32,162]{1,0:T(8,128)S(1)}, u32[]{:S(2)}, u32[]{:S(2)}) collective-permute-start(f32[32,162]{1,0:T(8,128)S(1)} %get-tuple-element.1343), channel_id=1, source_target_pairs={{0,4},{4,8},{8,12},{12,16},{16,20},{20,24},{24,28},{28,32},{32,36}... | collective-permute-start | bytes 62216 | tf_op jit(solution)/shard_map/while/body/eval_jaxpr/ppermute | solution.py:26
  129.3 19.4 %collective-permute-start.1 = (f32[32,162]{1,0:T(8,128)S(1)}, f32[32,162]{1,0:T(8,128)S(1)}, u32[]{:S(2)}, u32[]{:S(2)}) collective-permute-start(f32[32,162]{1,0:T(8,128)S(1)} %get-tuple-element.1343), channel_id=1, source_target_pairs={{0,4},{4,8},{8,12},{12,16},{16,20},{20,24},{24,28},{28,32},{32,36}... | collective-permute-start | bytes 62216 | tf_op jit(solution)/shard_map/while/body/eval_jaxpr/ppermute | solution.py:26
  149.8 4.2 collective-permute-start.1
  155.1 17.1 %collective-permute-start.1 = (f32[32,162]{1,0:T(8,128)S(1)}, f32[32,162]{1,0:T(8,128)S(1)}, u32[]{:S(2)}, u32[]{:S(2)}) collective-permute-start(f32[32,162]{1,0:T(8,128)S(1)} %get-tuple-element.1343), channel_id=1, source_target_pairs={{0,4},{4,8},{8,12},{12,16},{16,20},{20,24},{24,28},{28,32},{32,36}... | collective-permute-start | bytes 62216 | tf_op jit(solution)/shard_map/while/body/eval_jaxpr/ppermute | solution.py:26
  178.7 19.4 %collective-permute-start.1 = (f32[32,162]{1,0:T(8,128)S(1)}, f32[32,162]{1,0:T(8,128)S(1)}, u32[]{:S(2)}, u32[]{:S(2)}) collective-permute-start(f32[32,162]{1,0:T(8,128)S(1)} %get-tuple-element.1343), channel_id=1, source_target_pairs={{0,4},{4,8},{8,12},{12,16},{16,20},{20,24},{24,28},{28,32},{32,36}... | collective-permute-start | bytes 62216 | tf_op jit(solution)/shard_map/while/body/eval_jaxpr/ppermute | solution.py:26
  204.6 17.1 %collective-permute-start.1 = (f32[32,162]{1,0:T(8,128)S(1)}, f32[32,162]{1,0:T(8,128)S(1)}, u32[]{:S(2)}, u32[]{:S(2)}) collective-permute-start(f32[32,162]{1,0:T(8,128)S(1)} %get-tuple-element.1343), channel_id=1, source_target_pairs={{0,4},{4,8},{8,12},{12,16},{16,20},{20,24},{24,28},{28,32},{32,36}... | collective-permute-start | bytes 62216 | tf_op jit(solution)/shard_map/while/body/eval_jaxpr/ppermute | solution.py:26
  228.1 21.5 %collective-permute-start.1 = (f32[32,162]{1,0:T(8,128)S(1)}, f32[32,162]{1,0:T(8,128)S(1)}, u32[]{:S(2)}, u32[]{:S(2)}) collective-permute-start(f32[32,162]{1,0:T(8,128)S(1)} %get-tuple-element.1343), channel_id=1, source_target_pairs={{0,4},{4,8},{8,12},{12,16},{16,20},{20,24},{24,28},{28,32},{32,36}... | collective-permute-start | bytes 62216 | tf_op jit(solution)/shard_map/while/body/eval_jaxpr/ppermute | solution.py:26
  250.8 6.3 collective-permute-start.1
  258.2 15.0 %collective-permute-start.1 = (f32[32,162]{1,0:T(8,128)S(1)}, f32[32,162]{1,0:T(8,128)S(1)}, u32[]{:S(2)}, u32[]{:S(2)}) collective-permute-start(f32[32,162]{1,0:T(8,128)S(1)} %get-tuple-element.1343), channel_id=1, source_target_pairs={{0,4},{4,8},{8,12},{12,16},{16,20},{20,24},{24,28},{28,32},{32,36}... | collective-permute-start | bytes 62216 | tf_op jit(solution)/shard_map/while/body/eval_jaxpr/ppermute | solution.py:26
  274.3 6.3 collective-permute-start.1
  281.8 17.3 %collective-permute-start.1 = (f32[32,162]{1,0:T(8,128)S(1)}, f32[32,162]{1,0:T(8,128)S(1)}, u32[]{:S(2)}, u32[]{:S(2)}) collective-permute-start(f32[32,162]{1,0:T(8,128)S(1)} %get-tuple-element.1343), channel_id=1, source_target_pairs={{0,4},{4,8},{8,12},{12,16},{16,20},{20,24},{24,28},{28,32},{32,36}... | collective-permute-start | bytes 62216 | tf_op jit(solution)/shard_map/while/body/eval_jaxpr/ppermute | solution.py:26
  300.2 6.3 collective-permute-start.1
  307.6 15.0 %collective-permute-start.1 = (f32[32,162]{1,0:T(8,128)S(1)}, f32[32,162]{1,0:T(8,128)S(1)}, u32[]{:S(2)}, u32[]{:S(2)}) collective-permute-start(f32[32,162]{1,0:T(8,128)S(1)} %get-tuple-element.1343), channel_id=1, source_target_pairs={{0,4},{4,8},{8,12},{12,16},{16,20},{20,24},{24,28},{28,32},{32,36}... | collective-permute-start | bytes 62216 | tf_op jit(solution)/shard_map/while/body/eval_jaxpr/ppermute | solution.py:26
  323.7 6.3 collective-permute-start.1
  331.2 17.3 %collective-permute-start.1 = (f32[32,162]{1,0:T(8,128)S(1)}, f32[32,162]{1,0:T(8,128)S(1)}, u32[]{:S(2)}, u32[]{:S(2)}) collective-permute-start(f32[32,162]{1,0:T(8,128)S(1)} %get-tuple-element.1343), channel_id=1, source_target_pairs={{0,4},{4,8},{8,12},{12,16},{16,20},{20,24},{24,28},{28,32},{32,36}... | collective-permute-start | bytes 62216 | tf_op jit(solution)/shard_map/while/body/eval_jaxpr/ppermute | solution.py:26
  349.6 6.3 collective-permute-start.1
  357.0 15.0 %collective-permute-start.1 = (f32[32,162]{1,0:T(8,128)S(1)}, f32[32,162]{1,0:T(8,128)S(1)}, u32[]{:S(2)}, u32[]{:S(2)}) collective-permute-start(f32[32,162]{1,0:T(8,128)S(1)} %get-tuple-element.1343), channel_id=1, source_target_pairs={{0,4},{4,8},{8,12},{12,16},{16,20},{20,24},{24,28},{28,32},{32,36}... | collective-permute-start | bytes 62216 | tf_op jit(solution)/shard_map/while/body/eval_jaxpr/ppermute | solution.py:26
  373.2 6.3 collective-permute-start.1
  380.6 17.3 %collective-permute-start.1 = (f32[32,162]{1,0:T(8,128)S(1)}, f32[32,162]{1,0:T(8,128)S(1)}, u32[]{:S(2)}, u32[]{:S(2)}) collective-permute-start(f32[32,162]{1,0:T(8,128)S(1)} %get-tuple-element.1343), channel_id=1, source_target_pairs={{0,4},{4,8},{8,12},{12,16},{16,20},{20,24},{24,28},{28,32},{32,36}... | collective-permute-start | bytes 62216 | tf_op jit(solution)/shard_map/while/body/eval_jaxpr/ppermute | solution.py:26
  399.0 6.3 collective-permute-start.1
  406.4 15.0 %collective-permute-start.1 = (f32[32,162]{1,0:T(8,128)S(1)}, f32[32,162]{1,0:T(8,128)S(1)}, u32[]{:S(2)}, u32[]{:S(2)}) collective-permute-start(f32[32,162]{1,0:T(8,128)S(1)} %get-tuple-element.1343), channel_id=1, source_target_pairs={{0,4},{4,8},{8,12},{12,16},{16,20},{20,24},{24,28},{28,32},{32,36}... | collective-permute-start | bytes 62216 | tf_op jit(solution)/shard_map/while/body/eval_jaxpr/ppermute | solution.py:26
  422.6 6.3 collective-permute-start.1
  430.0 19.4 %collective-permute-start.1 = (f32[32,162]{1,0:T(8,128)S(1)}, f32[32,162]{1,0:T(8,128)S(1)}, u32[]{:S(2)}, u32[]{:S(2)}) collective-permute-start(f32[32,162]{1,0:T(8,128)S(1)} %get-tuple-element.1343), channel_id=1, source_target_pairs={{0,4},{4,8},{8,12},{12,16},{16,20},{20,24},{24,28},{28,32},{32,36}... | collective-permute-start | bytes 62216 | tf_op jit(solution)/shard_map/while/body/eval_jaxpr/ppermute | solution.py:26
  451.1 993.9 %while.105 = (s32[]{:T(128)}, f32[32,162]{1,0:T(8,128)S(1)}, f32[2,32,162]{2,1,0:T(8,128)}, s32[]{:T(128)}, f32[2,32,162]{2,1,0:T(8,128)}, /*index=5*/bf16[2,32,...) while((s32[]{:T(128)}, f32[32,162]{1,0:T(8,128)S(1)}, ...), condition=%wide.region_16.17_spmd.clone, body=%wide.region_11.16_spmd.clone.sunk | while | flops 20181448 | bytes 6007261 | solution.py:111
  453.1 6.0 collective-permute-done
  461.1 14.0 collective-permute-done
  477.1 6.0 collective-permute-done
  485.1 16.3 %collective-permute-done = f32[32,162]{1,0:T(8,128)S(1)} collective-permute-done((f32[32,162]{1,0:T(8,128)S(1)}, f32[32,162]{1,0:T(8,128)S(1)}, u32[]{:S(2)}, u32[]{:S(2)}) %collective-permute-start) | collective-permute-done | bytes 20768 | tf_op jit(solution)/shard_map/while/body/eval_jaxpr/ppermute | solution.py:26
  503.4 6.0 collective-permute-done
  511.4 14.0 collective-permute-done
  527.4 6.0 collective-permute-done
  535.4 16.2 %collective-permute-done = f32[32,162]{1,0:T(8,128)S(1)} collective-permute-done((f32[32,162]{1,0:T(8,128)S(1)}, f32[32,162]{1,0:T(8,128)S(1)}, u32[]{:S(2)}, u32[]{:S(2)}) %collective-permute-start) | collective-permute-done | bytes 20768 | tf_op jit(solution)/shard_map/while/body/eval_jaxpr/ppermute | solution.py:26
  553.7 6.0 collective-permute-done
  561.7 14.0 collective-permute-done
  577.7 6.0 collective-permute-done
  585.7 16.3 %collective-permute-done = f32[32,162]{1,0:T(8,128)S(1)} collective-permute-done((f32[32,162]{1,0:T(8,128)S(1)}, f32[32,162]{1,0:T(8,128)S(1)}, u32[]{:S(2)}, u32[]{:S(2)}) %collective-permute-start) | collective-permute-done | bytes 20768 | tf_op jit(solution)/shard_map/while/body/eval_jaxpr/ppermute | solution.py:26
  604.0 6.0 collective-permute-done
  612.0 14.0 collective-permute-done
  628.0 6.0 collective-permute-done
  636.0 18.3 %collective-permute-done = f32[32,162]{1,0:T(8,128)S(1)} collective-permute-done((f32[32,162]{1,0:T(8,128)S(1)}, f32[32,162]{1,0:T(8,128)S(1)}, u32[]{:S(2)}, u32[]{:S(2)}) %collective-permute-start) | collective-permute-done | bytes 20768 | tf_op jit(solution)/shard_map/while/body/eval_jaxpr/ppermute | solution.py:26
  656.4 6.0 collective-permute-done
  664.4 14.0 collective-permute-done
  680.4 6.0 collective-permute-done
  688.4 16.3 %collective-permute-done = f32[32,162]{1,0:T(8,128)S(1)} collective-permute-done((f32[32,162]{1,0:T(8,128)S(1)}, f32[32,162]{1,0:T(8,128)S(1)}, u32[]{:S(2)}, u32[]{:S(2)}) %collective-permute-start) | collective-permute-done | bytes 20768 | tf_op jit(solution)/shard_map/while/body/eval_jaxpr/ppermute | solution.py:26
  706.6 6.0 collective-permute-done
  714.7 14.0 collective-permute-done
  730.6 6.0 collective-permute-done
  738.7 16.2 %collective-permute-done = f32[32,162]{1,0:T(8,128)S(1)} collective-permute-done((f32[32,162]{1,0:T(8,128)S(1)}, f32[32,162]{1,0:T(8,128)S(1)}, u32[]{:S(2)}, u32[]{:S(2)}) %collective-permute-start) | collective-permute-done | bytes 20768 | tf_op jit(solution)/shard_map/while/body/eval_jaxpr/ppermute | solution.py:26
  756.9 5.4 collective-permute-done
  764.4 14.5 %collective-permute-done = f32[32,162]{1,0:T(8,128)S(1)} collective-permute-done((f32[32,162]{1,0:T(8,128)S(1)}, f32[32,162]{1,0:T(8,128)S(1)}, u32[]{:S(2)}, u32[]{:S(2)}) %collective-permute-start) | collective-permute-done | bytes 20768 | tf_op jit(solution)/shard_map/while/body/eval_jaxpr/ppermute | solution.py:26
  780.9 5.4 collective-permute-done
  788.3 16.8 %collective-permute-done = f32[32,162]{1,0:T(8,128)S(1)} collective-permute-done((f32[32,162]{1,0:T(8,128)S(1)}, f32[32,162]{1,0:T(8,128)S(1)}, u32[]{:S(2)}, u32[]{:S(2)}) %collective-permute-start) | collective-permute-done | bytes 20768 | tf_op jit(solution)/shard_map/while/body/eval_jaxpr/ppermute | solution.py:26
  807.2 5.4 collective-permute-done
  814.6 605.4 %collective-permute-done = f32[32,162]{1,0:T(8,128)S(1)} collective-permute-done((f32[32,162]{1,0:T(8,128)S(1)}, f32[32,162]{1,0:T(8,128)S(1)}, u32[]{:S(2)}, u32[]{:S(2)}) %collective-permute-start) | collective-permute-done | bytes 20768 | tf_op jit(solution)/shard_map/while/body/eval_jaxpr/ppermute | solution.py:26
  1420.2 19.6 %conditional.11 = (f32[2,32,162]{2,1,0:T(8,128)}, f32[32,162]{1,0:T(8,128)S(1)}) conditional(s32[]{:T(128)} %convert_element_type.80, f32[2,32,162]{2,1,0:T(8,128)} %get-tuple-element.1548, (f32[2,32]{1,0:T(2,128)S(1)}, f32[2,32,162]{2,1,0:T(8,128)}, bf16[2,32,162,162]{3,2,1,0:T(8,128)(2,1)}, bf16[2,32,162,162]{3,2,1,0:T(8,128)(2,1)}, ...), branch_computations={%region_12.12_spmd, %region_13.15_spmd} | conditional | flops 20165764 | bytes 5819981 | solution.py:104
  1420.8 19.0 %while.102 = (s32[]{:T(128)}, f32[32,162]{1,0:T(8,128)S(1)}, f32[2,32,162]{2,1,0:T(8,128)}, f32[2,32]{1,0:T(2,128)S(1)}, f32[2,32,162]{2,1,0:T(8,128)}, /*index=...) while((s32[]{:T(128)}, f32[32,162]{1,0:T(8,128)S(1)}, ...), condition=%wide.region_15.14_spmd, body=%wide.region_14.13_spmd.sunk | while | flops 20165764 | bytes 5736945 | solution.py:95
  (440 shorter events, 175.4 us)
Async XLA Ops:
  0.0 33.3 %collective-permute-start.2 = (bf16[64,162]{1,0:T(8,128)(2,1)}, bf16[64,162]{1,0:T(8,128)(2,1)S(1)}, u32[]{:S(2)}, u32[]{:S(2)}) collective-permute-start(bf16[64,162]{1,0:T(8,128)(2,1)} %param.30), channel_id=1, source_target_pairs={{0,1},{1,2},{2,3},{3,0},{4,5},{5,6},{6,7},{7,4},{8,9},{9,10},{10,1... | collective-permute-start | bytes 62216 | tf_op jit(solution)/shard_map/ppermute | solution.py:14
  2.5 30.8 %collective-permute-start.3 = (bf16[64,162]{1,0:T(8,128)(2,1)}, bf16[64,162]{1,0:T(8,128)(2,1)S(1)}, u32[]{:S(2)}, u32[]{:S(2)}) collective-permute-start(bf16[64,162]{1,0:T(8,128)(2,1)} %param.30), channel_id=1, source_target_pairs={{1,0},{2,1},{3,2},{0,3},{5,4},{6,5},{7,6},{4,7},{9,8},{10,9},{11,1... | collective-permute-start | bytes 62216 | tf_op jit(solution)/shard_map/ppermute | solution.py:16
  36.5 20.4 %collective-permute-start.1 = (f32[32,162]{1,0:T(8,128)S(1)}, f32[32,162]{1,0:T(8,128)S(1)}, u32[]{:S(2)}, u32[]{:S(2)}) collective-permute-start(f32[32,162]{1,0:T(8,128)S(1)} %get-tuple-element.1343), channel_id=1, source_target_pairs={{0,4},{4,8},{8,12},{12,16},{16,20},{20,24},{24,28},{28,32},{32,36}... | collective-permute-start | bytes 62216 | tf_op jit(solution)/shard_map/while/body/eval_jaxpr/ppermute | solution.py:26
  74.5 3.1 collective-permute-start.1
  77.7 22.6 %collective-permute-start.1 = (f32[32,162]{1,0:T(8,128)S(1)}, f32[32,162]{1,0:T(8,128)S(1)}, u32[]{:S(2)}, u32[]{:S(2)}) collective-permute-start(f32[32,162]{1,0:T(8,128)S(1)} %get-tuple-element.1343), channel_id=1, source_target_pairs={{0,4},{4,8},{8,12},{12,16},{16,20},{20,24},{24,28},{28,32},{32,36}... | collective-permute-start | bytes 62216 | tf_op jit(solution)/shard_map/while/body/eval_jaxpr/ppermute | solution.py:26
  100.4 5.2 collective-permute-start.1
  105.7 18.2 %collective-permute-start.1 = (f32[32,162]{1,0:T(8,128)S(1)}, f32[32,162]{1,0:T(8,128)S(1)}, u32[]{:S(2)}, u32[]{:S(2)}) collective-permute-start(f32[32,162]{1,0:T(8,128)S(1)} %get-tuple-element.1343), channel_id=1, source_target_pairs={{0,4},{4,8},{8,12},{12,16},{16,20},{20,24},{24,28},{28,32},{32,36}... | collective-permute-start | bytes 62216 | tf_op jit(solution)/shard_map/while/body/eval_jaxpr/ppermute | solution.py:26
  124.0 5.2 collective-permute-start.1
  129.3 20.4 %collective-permute-start.1 = (f32[32,162]{1,0:T(8,128)S(1)}, f32[32,162]{1,0:T(8,128)S(1)}, u32[]{:S(2)}, u32[]{:S(2)}) collective-permute-start(f32[32,162]{1,0:T(8,128)S(1)} %get-tuple-element.1343), channel_id=1, source_target_pairs={{0,4},{4,8},{8,12},{12,16},{16,20},{20,24},{24,28},{28,32},{32,36}... | collective-permute-start | bytes 62216 | tf_op jit(solution)/shard_map/while/body/eval_jaxpr/ppermute | solution.py:26
  149.8 5.2 collective-permute-start.1
  155.1 18.1 %collective-permute-start.1 = (f32[32,162]{1,0:T(8,128)S(1)}, f32[32,162]{1,0:T(8,128)S(1)}, u32[]{:S(2)}, u32[]{:S(2)}) collective-permute-start(f32[32,162]{1,0:T(8,128)S(1)} %get-tuple-element.1343), channel_id=1, source_target_pairs={{0,4},{4,8},{8,12},{12,16},{16,20},{20,24},{24,28},{28,32},{32,36}... | collective-permute-start | bytes 62216 | tf_op jit(solution)/shard_map/while/body/eval_jaxpr/ppermute | solution.py:26
  173.4 5.2 collective-permute-start.1
  178.7 20.4 %collective-permute-start.1 = (f32[32,162]{1,0:T(8,128)S(1)}, f32[32,162]{1,0:T(8,128)S(1)}, u32[]{:S(2)}, u32[]{:S(2)}) collective-permute-start(f32[32,162]{1,0:T(8,128)S(1)} %get-tuple-element.1343), channel_id=1, source_target_pairs={{0,4},{4,8},{8,12},{12,16},{16,20},{20,24},{24,28},{28,32},{32,36}... | collective-permute-start | bytes 62216 | tf_op jit(solution)/shard_map/while/body/eval_jaxpr/ppermute | solution.py:26
  199.2 5.2 collective-permute-start.1
  204.6 18.1 %collective-permute-start.1 = (f32[32,162]{1,0:T(8,128)S(1)}, f32[32,162]{1,0:T(8,128)S(1)}, u32[]{:S(2)}, u32[]{:S(2)}) collective-permute-start(f32[32,162]{1,0:T(8,128)S(1)} %get-tuple-element.1343), channel_id=1, source_target_pairs={{0,4},{4,8},{8,12},{12,16},{16,20},{20,24},{24,28},{28,32},{32,36}... | collective-permute-start | bytes 62216 | tf_op jit(solution)/shard_map/while/body/eval_jaxpr/ppermute | solution.py:26
  222.8 5.2 collective-permute-start.1
  228.1 22.6 %collective-permute-start.1 = (f32[32,162]{1,0:T(8,128)S(1)}, f32[32,162]{1,0:T(8,128)S(1)}, u32[]{:S(2)}, u32[]{:S(2)}) collective-permute-start(f32[32,162]{1,0:T(8,128)S(1)} %get-tuple-element.1343), channel_id=1, source_target_pairs={{0,4},{4,8},{8,12},{12,16},{16,20},{20,24},{24,28},{28,32},{32,36}... | collective-permute-start | bytes 62216 | tf_op jit(solution)/shard_map/while/body/eval_jaxpr/ppermute | solution.py:26
  250.8 7.3 collective-permute-start.1
  258.2 16.0 %collective-permute-start.1 = (f32[32,162]{1,0:T(8,128)S(1)}, f32[32,162]{1,0:T(8,128)S(1)}, u32[]{:S(2)}, u32[]{:S(2)}) collective-permute-start(f32[32,162]{1,0:T(8,128)S(1)} %get-tuple-element.1343), channel_id=1, source_target_pairs={{0,4},{4,8},{8,12},{12,16},{16,20},{20,24},{24,28},{28,32},{32,36}... | collective-permute-start | bytes 62216 | tf_op jit(solution)/shard_map/while/body/eval_jaxpr/ppermute | solution.py:26
  274.3 7.3 collective-permute-start.1
  281.8 18.3 %collective-permute-start.1 = (f32[32,162]{1,0:T(8,128)S(1)}, f32[32,162]{1,0:T(8,128)S(1)}, u32[]{:S(2)}, u32[]{:S(2)}) collective-permute-start(f32[32,162]{1,0:T(8,128)S(1)} %get-tuple-element.1343), channel_id=1, source_target_pairs={{0,4},{4,8},{8,12},{12,16},{16,20},{20,24},{24,28},{28,32},{32,36}... | collective-permute-start | bytes 62216 | tf_op jit(solution)/shard_map/while/body/eval_jaxpr/ppermute | solution.py:26
  300.2 7.3 collective-permute-start.1
  307.6 16.0 %collective-permute-start.1 = (f32[32,162]{1,0:T(8,128)S(1)}, f32[32,162]{1,0:T(8,128)S(1)}, u32[]{:S(2)}, u32[]{:S(2)}) collective-permute-start(f32[32,162]{1,0:T(8,128)S(1)} %get-tuple-element.1343), channel_id=1, source_target_pairs={{0,4},{4,8},{8,12},{12,16},{16,20},{20,24},{24,28},{28,32},{32,36}... | collective-permute-start | bytes 62216 | tf_op jit(solution)/shard_map/while/body/eval_jaxpr/ppermute | solution.py:26
  323.7 7.3 collective-permute-start.1
  331.2 18.3 %collective-permute-start.1 = (f32[32,162]{1,0:T(8,128)S(1)}, f32[32,162]{1,0:T(8,128)S(1)}, u32[]{:S(2)}, u32[]{:S(2)}) collective-permute-start(f32[32,162]{1,0:T(8,128)S(1)} %get-tuple-element.1343), channel_id=1, source_target_pairs={{0,4},{4,8},{8,12},{12,16},{16,20},{20,24},{24,28},{28,32},{32,36}... | collective-permute-start | bytes 62216 | tf_op jit(solution)/shard_map/while/body/eval_jaxpr/ppermute | solution.py:26
  349.6 7.3 collective-permute-start.1
  357.0 16.0 %collective-permute-start.1 = (f32[32,162]{1,0:T(8,128)S(1)}, f32[32,162]{1,0:T(8,128)S(1)}, u32[]{:S(2)}, u32[]{:S(2)}) collective-permute-start(f32[32,162]{1,0:T(8,128)S(1)} %get-tuple-element.1343), channel_id=1, source_target_pairs={{0,4},{4,8},{8,12},{12,16},{16,20},{20,24},{24,28},{28,32},{32,36}... | collective-permute-start | bytes 62216 | tf_op jit(solution)/shard_map/while/body/eval_jaxpr/ppermute | solution.py:26
  373.2 7.3 collective-permute-start.1
  380.6 18.3 %collective-permute-start.1 = (f32[32,162]{1,0:T(8,128)S(1)}, f32[32,162]{1,0:T(8,128)S(1)}, u32[]{:S(2)}, u32[]{:S(2)}) collective-permute-start(f32[32,162]{1,0:T(8,128)S(1)} %get-tuple-element.1343), channel_id=1, source_target_pairs={{0,4},{4,8},{8,12},{12,16},{16,20},{20,24},{24,28},{28,32},{32,36}... | collective-permute-start | bytes 62216 | tf_op jit(solution)/shard_map/while/body/eval_jaxpr/ppermute | solution.py:26
  399.0 7.3 collective-permute-start.1
  406.4 16.0 %collective-permute-start.1 = (f32[32,162]{1,0:T(8,128)S(1)}, f32[32,162]{1,0:T(8,128)S(1)}, u32[]{:S(2)}, u32[]{:S(2)}) collective-permute-start(f32[32,162]{1,0:T(8,128)S(1)} %get-tuple-element.1343), channel_id=1, source_target_pairs={{0,4},{4,8},{8,12},{12,16},{16,20},{20,24},{24,28},{28,32},{32,36}... | collective-permute-start | bytes 62216 | tf_op jit(solution)/shard_map/while/body/eval_jaxpr/ppermute | solution.py:26
  422.6 7.3 collective-permute-start.1
  430.0 20.4 %collective-permute-start.1 = (f32[32,162]{1,0:T(8,128)S(1)}, f32[32,162]{1,0:T(8,128)S(1)}, u32[]{:S(2)}, u32[]{:S(2)}) collective-permute-start(f32[32,162]{1,0:T(8,128)S(1)} %get-tuple-element.1343), channel_id=1, source_target_pairs={{0,4},{4,8},{8,12},{12,16},{16,20},{20,24},{24,28},{28,32},{32,36}... | collective-permute-start | bytes 62216 | tf_op jit(solution)/shard_map/while/body/eval_jaxpr/ppermute | solution.py:26
  451.2 7.9 collective-permute-start
  459.2 15.9 %collective-permute-start = (f32[32,162]{1,0:T(8,128)S(1)}, f32[32,162]{1,0:T(8,128)S(1)}, u32[]{:S(2)}, u32[]{:S(2)}) collective-permute-start(f32[32,162]{1,0:T(8,128)S(1)} %get-tuple-element.1354), channel_id=1, source_target_pairs={{4,0},{8,4},{12,8},{16,12},{20,16},{24,20},{28,24},{32,28},{36,32}... | collective-permute-start | bytes 62216 | tf_op jit(solution)/shard_map/while/body/eval_jaxpr/ppermute | solution.py:26
  475.2 7.9 collective-permute-start
  483.2 18.2 %collective-permute-start = (f32[32,162]{1,0:T(8,128)S(1)}, f32[32,162]{1,0:T(8,128)S(1)}, u32[]{:S(2)}, u32[]{:S(2)}) collective-permute-start(f32[32,162]{1,0:T(8,128)S(1)} %get-tuple-element.1354), channel_id=1, source_target_pairs={{4,0},{8,4},{12,8},{16,12},{20,16},{24,20},{28,24},{32,28},{36,32}... | collective-permute-start | bytes 62216 | tf_op jit(solution)/shard_map/while/body/eval_jaxpr/ppermute | solution.py:26
  501.5 7.9 collective-permute-start
  509.5 15.9 %collective-permute-start = (f32[32,162]{1,0:T(8,128)S(1)}, f32[32,162]{1,0:T(8,128)S(1)}, u32[]{:S(2)}, u32[]{:S(2)}) collective-permute-start(f32[32,162]{1,0:T(8,128)S(1)} %get-tuple-element.1354), channel_id=1, source_target_pairs={{4,0},{8,4},{12,8},{16,12},{20,16},{24,20},{28,24},{32,28},{36,32}... | collective-permute-start | bytes 62216 | tf_op jit(solution)/shard_map/while/body/eval_jaxpr/ppermute | solution.py:26
  525.5 7.9 collective-permute-start
  533.5 18.2 %collective-permute-start = (f32[32,162]{1,0:T(8,128)S(1)}, f32[32,162]{1,0:T(8,128)S(1)}, u32[]{:S(2)}, u32[]{:S(2)}) collective-permute-start(f32[32,162]{1,0:T(8,128)S(1)} %get-tuple-element.1354), channel_id=1, source_target_pairs={{4,0},{8,4},{12,8},{16,12},{20,16},{24,20},{28,24},{32,28},{36,32}... | collective-permute-start | bytes 62216 | tf_op jit(solution)/shard_map/while/body/eval_jaxpr/ppermute | solution.py:26
  551.8 7.9 collective-permute-start
  559.8 15.9 %collective-permute-start = (f32[32,162]{1,0:T(8,128)S(1)}, f32[32,162]{1,0:T(8,128)S(1)}, u32[]{:S(2)}, u32[]{:S(2)}) collective-permute-start(f32[32,162]{1,0:T(8,128)S(1)} %get-tuple-element.1354), channel_id=1, source_target_pairs={{4,0},{8,4},{12,8},{16,12},{20,16},{24,20},{28,24},{32,28},{36,32}... | collective-permute-start | bytes 62216 | tf_op jit(solution)/shard_map/while/body/eval_jaxpr/ppermute | solution.py:26
  575.7 7.9 collective-permute-start
  583.8 18.2 %collective-permute-start = (f32[32,162]{1,0:T(8,128)S(1)}, f32[32,162]{1,0:T(8,128)S(1)}, u32[]{:S(2)}, u32[]{:S(2)}) collective-permute-start(f32[32,162]{1,0:T(8,128)S(1)} %get-tuple-element.1354), channel_id=1, source_target_pairs={{4,0},{8,4},{12,8},{16,12},{20,16},{24,20},{28,24},{32,28},{36,32}... | collective-permute-start | bytes 62216 | tf_op jit(solution)/shard_map/while/body/eval_jaxpr/ppermute | solution.py:26
  602.0 7.9 collective-permute-start
  610.0 15.9 %collective-permute-start = (f32[32,162]{1,0:T(8,128)S(1)}, f32[32,162]{1,0:T(8,128)S(1)}, u32[]{:S(2)}, u32[]{:S(2)}) collective-permute-start(f32[32,162]{1,0:T(8,128)S(1)} %get-tuple-element.1354), channel_id=1, source_target_pairs={{4,0},{8,4},{12,8},{16,12},{20,16},{24,20},{28,24},{32,28},{36,32}... | collective-permute-start | bytes 62216 | tf_op jit(solution)/shard_map/while/body/eval_jaxpr/ppermute | solution.py:26
  626.0 7.9 collective-permute-start
  634.1 20.3 %collective-permute-start = (f32[32,162]{1,0:T(8,128)S(1)}, f32[32,162]{1,0:T(8,128)S(1)}, u32[]{:S(2)}, u32[]{:S(2)}) collective-permute-start(f32[32,162]{1,0:T(8,128)S(1)} %get-tuple-element.1354), channel_id=1, source_target_pairs={{4,0},{8,4},{12,8},{16,12},{20,16},{24,20},{28,24},{32,28},{36,32}... | collective-permute-start | bytes 62216 | tf_op jit(solution)/shard_map/while/body/eval_jaxpr/ppermute | solution.py:26
  654.4 7.9 collective-permute-start
  662.4 15.9 %collective-permute-start = (f32[32,162]{1,0:T(8,128)S(1)}, f32[32,162]{1,0:T(8,128)S(1)}, u32[]{:S(2)}, u32[]{:S(2)}) collective-permute-start(f32[32,162]{1,0:T(8,128)S(1)} %get-tuple-element.1354), channel_id=1, source_target_pairs={{4,0},{8,4},{12,8},{16,12},{20,16},{24,20},{28,24},{32,28},{36,32}... | collective-permute-start | bytes 62216 | tf_op jit(solution)/shard_map/while/body/eval_jaxpr/ppermute | solution.py:26
  678.4 7.9 collective-permute-start
  686.4 18.2 %collective-permute-start = (f32[32,162]{1,0:T(8,128)S(1)}, f32[32,162]{1,0:T(8,128)S(1)}, u32[]{:S(2)}, u32[]{:S(2)}) collective-permute-start(f32[32,162]{1,0:T(8,128)S(1)} %get-tuple-element.1354), channel_id=1, source_target_pairs={{4,0},{8,4},{12,8},{16,12},{20,16},{24,20},{28,24},{32,28},{36,32}... | collective-permute-start | bytes 62216 | tf_op jit(solution)/shard_map/while/body/eval_jaxpr/ppermute | solution.py:26
  704.7 7.9 collective-permute-start
  712.7 15.9 %collective-permute-start = (f32[32,162]{1,0:T(8,128)S(1)}, f32[32,162]{1,0:T(8,128)S(1)}, u32[]{:S(2)}, u32[]{:S(2)}) collective-permute-start(f32[32,162]{1,0:T(8,128)S(1)} %get-tuple-element.1354), channel_id=1, source_target_pairs={{4,0},{8,4},{12,8},{16,12},{20,16},{24,20},{28,24},{32,28},{36,32}... | collective-permute-start | bytes 62216 | tf_op jit(solution)/shard_map/while/body/eval_jaxpr/ppermute | solution.py:26
  728.7 7.9 collective-permute-start
  736.7 18.2 %collective-permute-start = (f32[32,162]{1,0:T(8,128)S(1)}, f32[32,162]{1,0:T(8,128)S(1)}, u32[]{:S(2)}, u32[]{:S(2)}) collective-permute-start(f32[32,162]{1,0:T(8,128)S(1)} %get-tuple-element.1354), channel_id=1, source_target_pairs={{4,0},{8,4},{12,8},{16,12},{20,16},{24,20},{28,24},{32,28},{36,32}... | collective-permute-start | bytes 62216 | tf_op jit(solution)/shard_map/while/body/eval_jaxpr/ppermute | solution.py:26
  755.0 7.3 collective-permute-start
  762.4 16.5 %collective-permute-start = (f32[32,162]{1,0:T(8,128)S(1)}, f32[32,162]{1,0:T(8,128)S(1)}, u32[]{:S(2)}, u32[]{:S(2)}) collective-permute-start(f32[32,162]{1,0:T(8,128)S(1)} %get-tuple-element.1354), channel_id=1, source_target_pairs={{4,0},{8,4},{12,8},{16,12},{20,16},{24,20},{28,24},{32,28},{36,32}... | collective-permute-start | bytes 62216 | tf_op jit(solution)/shard_map/while/body/eval_jaxpr/ppermute | solution.py:26
  779.0 7.3 collective-permute-start
  786.4 18.8 %collective-permute-start = (f32[32,162]{1,0:T(8,128)S(1)}, f32[32,162]{1,0:T(8,128)S(1)}, u32[]{:S(2)}, u32[]{:S(2)}) collective-permute-start(f32[32,162]{1,0:T(8,128)S(1)} %get-tuple-element.1354), channel_id=1, source_target_pairs={{4,0},{8,4},{12,8},{16,12},{20,16},{24,20},{28,24},{32,28},{36,32}... | collective-permute-start | bytes 62216 | tf_op jit(solution)/shard_map/while/body/eval_jaxpr/ppermute | solution.py:26
  805.3 7.3 collective-permute-start
  812.7 607.3 %collective-permute-start = (f32[32,162]{1,0:T(8,128)S(1)}, f32[32,162]{1,0:T(8,128)S(1)}, u32[]{:S(2)}, u32[]{:S(2)}) collective-permute-start(f32[32,162]{1,0:T(8,128)S(1)} %get-tuple-element.1354), channel_id=1, source_target_pairs={{4,0},{8,4},{12,8},{16,12},{20,16},{24,20},{28,24},{32,28},{36,32}... | collective-permute-start | bytes 62216 | tf_op jit(solution)/shard_map/while/body/eval_jaxpr/ppermute | solution.py:26
  1439.8 5.2 collective-permute-start
  (5 other events, 63.6 us)
where the time goes:
time: 1470 us; the launch traced here: 1450 us
  waiting for transfers between devices  958 us (65%)
  starting transfers between devices  411 us (28%)
  matrix products  32.2 us (2%)
  local copies, waits for them, and re-layouts  28.4 us (2%)
    ppermute x62, waiting for transfers between devices, passed_along(): return lax.ppermute(block, axis, route)  958 us
    ppermute x62, starting transfers between devices, passed_along(): return lax.ppermute(block, axis, route)  406 us
    dot_general x8, matrix products, apply_block(): jnp.einsum('lij,lj->li', matrix.astype(jnp.float32), vector, precision=la...  32.1 us
  transfers between devices with their start and end apart: 64, of which 62 were waited for; matrix products, arithmetic and copies ran while one was open for 2% of the time, Pallas kernels for 0%

commit v1 on v0

v1 whole, which is shorter than its diff:
```python
import functools

import jax
import jax.numpy as jnp
from jax import lax
from jax.experimental import pallas as pl
from jax.experimental.pallas import tpu as pltpu
from jax.sharding import PartitionSpec as P

MESH = pl.DeviceIdType.MESH
NT = (((1,), (1,)), ((), ()))
TN = (((0,), (0,)), ((), ()))
F32 = jnp.float32
BF = jnp.bfloat16
B = 162
TAIL = B - 128
CHUNK = 56
CODED = 168 + CHUNK
TOP = 32512.0


def dot(a, b):
    return jnp.dot(a, b, preferred_element_type=F32)


def halves(m):
    hi = m.astype(BF)
    return hi, (m - hi.astype(F32)).astype(BF)


def product(a, b):
    ah, al = halves(a)
    bh, bl = halves(b)
    return dot(ah, bh) + (dot(ah, bl) + dot(al, bh))


def two_rows(v):
    row = lax.broadcasted_iota(jnp.int32, v.shape, 0)
    hi = v.astype(BF).astype(F32)
    return jnp.where(row % 2 == 0, hi, v - hi).astype(BF)


def apply_map(matrix, v):
    out = lax.dot_general(two_rows(v), matrix, NT, preferred_element_type=F32)
    return out + pltpu.roll(out, 1, 0)


def wide(row):
    return jnp.broadcast_to(row, (8, B))


def kernel(
    state_ref, source_ref, coef_ref, nbr_ref, lift_ref, slot_ref, len_ref, d_hbm, l_hbm, u_hbm,
    out_ref,
    d_raw, l_raw, u_raw, wide_s, d_mat, l_mat, u_mat, ext, rhs, tail_s,
    send_a, recv_a, vec_a, got_vec_a, send_b, recv_b, vec_b, got_vec_b,
    map_h, map_l, y_s, c_out, c_in, e_out, e_in, x_out, x_in,
    load_sem, ext_ss, ext_rs, a_ss, a_rs, va_ss, va_rs, b_ss, b_rs, vb_ss, vb_rs,
    c_ss, c_rs, e_ss, e_rs, x_ss, x_rs,
):
    me = lax.axis_index("wall")
    surf = lax.axis_index("surf")
    wall_count = send_a.shape[0]
    lines = wall_count
    surf_count = lax.axis_size("surf")

    def dev(w):
        return (w, surf)

    loads = ((d_hbm, d_raw), (l_hbm, l_raw), (u_hbm, u_raw))

    def load(k, e, b):
        src, dst = loads[k]
        return pltpu.make_async_copy(
            src.at[e, :, pl.ds(pl.multiple_of(8 * b, 8), 8), :], dst.at[e, b], load_sem.at[k, e, b]
        )

    for b in range(4):
        for k in range(2):
            for e in range(2):
                load(k, e, b).start()
    for b in range(4):
        for e in range(2):
            load(2, e, b).start()

    barrier = pltpu.get_barrier_semaphore()
    after = lax.rem(surf + 1, surf_count)
    before = lax.rem(surf + surf_count - 1, surf_count)
    for s in (after, before):
        pl.semaphore_signal(barrier, inc=1, device_id=(me, s), device_id_type=MESH)

    @pl.loop(0, wall_count)
    def _(w):
        @pl.when(w != me)
        def _():
            pl.semaphore_signal(barrier, inc=1, device_id=dev(w), device_id_type=MESH)

    pl.semaphore_wait(barrier, wall_count - 1 + 2)

    halo = []
    for k, (s, place) in enumerate(((after, 0), (before, 2))):
        copy = pltpu.make_async_remote_copy(
            src_ref=state_ref, dst_ref=ext.at[place], send_sem=ext_ss.at[k], recv_sem=ext_rs.at[k],
            device_id=(me, s), device_id_type=MESH,
        )
        copy.start()
        halo.append(copy)
    ext[1] = state_ref[...]
    tail_s[...] = jnp.zeros_like(tail_s)

    kpos = lax.broadcasted_iota(jnp.int32, (192, 64), 0)
    own = kpos == 64 + lax.broadcasted_iota(jnp.int32, (192, 64), 1)
    weight = jnp.zeros((192, 64), F32)
    for f in range(4):
        hit = kpos == nbr_ref[pl.ds(f, 1), :]
        weight = weight + coef_ref[pl.ds(f, 1), :] * (own.astype(F32) - hit.astype(F32))
    for copy in halo:
        copy.wait()
    w1 = weight.astype(BF)
    rest = weight - w1.astype(F32)
    w2 = rest.astype(BF)
    w3 = (rest - w2.astype(F32)).astype(BF)
    cells = ext[...].reshape(192, B)
    face_sum = sum(
        lax.dot_general(w, cells, TN, preferred_element_type=F32) for w in (w3, w2, w1)
    ).astype(BF)
    spos = lax.broadcasted_iota(jnp.int32, (64, 32), 0)
    for e in range(2):
        pick = (spos == slot_ref[pl.ds(e, 1), :]).astype(F32).astype(BF)
        faces = lax.dot_general(pick, face_sum, TN, preferred_element_type=F32).astype(BF)
        mine = lax.dot_general(pick, source_ref[...], TN, preferred_element_type=F32)
        rhs[e] = mine - dot(faces, lift_ref[...])

    def active(e, l):
        return jnp.where(2 * me + e < len_ref[l], 1.0, 0.0).astype(F32)

    def widen(k, slot, e, b):
        raw = loads[k][1]

        @pl.loop(0, 9)
        def _(i):
            v = raw[e, b, pl.ds(i * 18, 18)].astype(F32)
            rows = pl.ds(pl.multiple_of(i * 144, 8), 144)
            wide_s[slot, 0, rows, :] = v[:, :, :128].reshape(144, 128)
            wide_s[slot, 1, rows, pl.ds(0, TAIL)] = v[:, :, 128:].reshape(144, TAIL)

    def one_line(slot, u, dst, e, l):
        dst[e, l, :, pl.ds(0, 128)] = wide_s[slot, 0, pl.ds(u, B, stride=8), :].astype(BF)
        high = wide_s[slot, 1, pl.ds(u, B, stride=8), :]
        dst[e, l, :, pl.ds(128, TAIL)] = high[:, :TAIL].astype(BF)

    def encode(m, store, vec, l, t):
        top = jnp.max(jnp.abs(m), axis=0, keepdims=True)
        inv = jnp.where(top > 0.0, TOP / jnp.where(top > 0.0, top, 1.0), 0.0)
        vec[l, pl.ds(1, 1), :] = top * (1.0 / TOP)
        q = jnp.floor(m * inv + 0.5)
        store[l, pl.ds(0, B), :] = q[:, :128].astype(jnp.int32).astype(jnp.int16)
        tail_s[t, pl.ds(0, B), pl.ds(0, TAIL)] = q[:, 128:]
        packed = tail_s[t, pl.ds(0, CHUNK), :]
        packed = packed + pltpu.roll(tail_s[t, pl.ds(CHUNK, CHUNK), :], 42, 1)
        packed = packed + pltpu.roll(tail_s[t, pl.ds(2 * CHUNK, CHUNK), :], 84, 1)
        store[l, pl.ds(168, CHUNK), :] = packed.astype(jnp.int32).astype(jnp.int16)

    def decode(coded, d, t):
        def split(q):
            v = q.astype(jnp.int32).astype(F32)
            hi = jnp.floor(v * (1.0 / 256.0) + 0.5)
            return hi, v - 256.0 * hi

        hi, lo = split(coded[d, pl.ds(0, B), :])
        map_h[d, :, pl.ds(0, 128)] = hi.astype(BF)
        map_l[d, :, pl.ds(0, 128)] = lo.astype(BF)
        packed = coded[d, pl.ds(168, CHUNK), :].astype(jnp.int32).astype(F32)
        for k, shift in ((0, 0), (1, 128 - 42), (2, 128 - 84)):
            part = packed if shift == 0 else pltpu.roll(packed, shift, 1)
            tail_s[t, pl.ds(k * CHUNK, CHUNK), pl.ds(0, TAIL)] = part[:, :TAIL]
        v = tail_s[t, pl.ds(0, B), :][:, :TAIL]
        hi = jnp.floor(v * (1.0 / 256.0) + 0.5)
        map_h[d, :, pl.ds(128, TAIL)] = hi.astype(BF)
        map_l[d, :, pl.ds(128, TAIL)] = (v - 256.0 * hi).astype(BF)

    def apply_coded(d, scale, v):
        rows = two_rows(v * scale)
        out = 256.0 * lax.dot_general(rows, map_h[d], NT, preferred_element_type=F32)
        out = out + lax.dot_general(rows, map_l[d], NT, preferred_element_type=F32)
        return out + pltpu.roll(out, 1, 0)

    def post(src, dst, ss, rs, to):
        return pltpu.make_async_remote_copy(
            src_ref=src.at[to], dst_ref=dst.at[me], send_sem=ss.at[to], recv_sem=rs.at[me],
            device_id=dev(to), device_id_type=MESH,
        )

    def arrive(src, dst, ss, rs, frm):
        pltpu.make_async_remote_copy(
            src_ref=src.at[frm], dst_ref=dst.at[frm], send_sem=ss.at[frm], recv_sem=rs.at[frm],
            device_id=dev(frm), device_id_type=MESH,
        ).wait_recv()

    def deliver(src, dst, ss, rs, to):
        @pl.when(to != me)
        def _():
            post(src, dst, ss, rs, to).start()

        @pl.when(to == me)
        def _():
            dst[me] = src[me]

    def expect(src, dst, ss, rs, frm):
        @pl.when(frm != me)
        def _():
            arrive(src, dst, ss, rs, frm)

    msg_a = (send_a, recv_a, a_ss, a_rs)
    msg_va = (vec_a, got_vec_a, va_ss, va_rs)
    msg_b = (send_b, recv_b, b_ss, b_rs)
    msg_vb = (vec_b, got_vec_b, vb_ss, vb_rs)
    msg_c = (c_out, c_in, c_ss, c_rs)
    msg_e = (e_out, e_in, e_ss, e_rs)
    msg_x = (x_out, x_in, x_ss, x_rs)

    @pl.loop(0, 4)
    def _(b):
        for k in range(2):
            for e in range(2):
                load(k, e, b).wait()
                widen(k, 2 * k + e, e, b)

        @pl.loop(0, 4)
        def _(half):
            for t in range(2):
                u = 2 * half + t
                l = 8 * b + u
                for e in range(2):
                    one_line(e, u, d_mat, e, l)
                    one_line(2 + e, u, l_mat, e, l)
                first = active(0, l) * dot(d_mat[0, l], l_mat[0, l])
                second = active(1, l) * dot(d_mat[1, l], l_mat[1, l])
                encode(product(second, first), send_a, vec_a, l, t)
                y = active(0, l) * apply_map(d_mat[0, l], wide(rhs[0, pl.ds(l, 1), :]))
                y = wide(rhs[1, pl.ds(l, 1), :]) - apply_map(l_mat[1, l], y)
                y = active(1, l) * apply_map(d_mat[1, l], y)
                vec_a[l, pl.ds(0, 1), :] = y[:1]
            for t in range(2):
                l = 8 * b + 2 * half + t
                deliver(*msg_a, l)
                deliver(*msg_va, l)

    @pl.loop(0, 4)
    def _(b):
        for e in range(2):
            load(2, e, b).wait()
            widen(2, e, e, b)

        @pl.loop(0, 4)
        def _(half):
            for t in range(2):
                u = 2 * half + t
                l = 8 * b + u
                for e in range(2):
                    one_line(e, u, u_mat, e, l)
                first = active(0, l) * dot(d_mat[0, l], u_mat[0, l])
                second = active(1, l) * dot(d_mat[1, l], u_mat[1, l])
                encode(product(first, second), send_b, vec_b, l, t)
                vec_b[l, pl.ds(0, 1), :] = jnp.zeros((1, B), F32)

    @pl.loop(0, wall_count // 2)
    def _(i):
        for t in range(2):
            expect(*msg_a, 2 * i + t)
            expect(*msg_va, 2 * i + t)
        for t in range(2):
            decode(recv_a, 2 * i + t, t)

    @pl.loop(0, wall_count)
    def _(l):
        deliver(*msg_b, l)
        deliver(*msg_vb, l)

    def fwd(d, v):
        c_out[d] = v[:1]
        deliver(*msg_c, d)
        got = got_vec_a[d]
        return apply_coded(d, wide(got[1:2]), v) + wide(got[0:1])

    lax.fori_loop(0, wall_count, fwd, jnp.zeros((8, B), F32))

    @pl.loop(0, lines // 4)
    def _(i):
        for t in range(4):
            expect(*msg_c, 4 * i + t)
        for t in range(4):
            l = 4 * i + t
            v = wide(rhs[0, pl.ds(l, 1), :]) - apply_map(l_mat[0, l], wide(c_in[l]))
            y1 = active(0, l) * apply_map(d_mat[0, l], v)
            v = wide(rhs[1, pl.ds(l, 1), :]) - apply_map(l_mat[1, l], y1)
            y2 = active(1, l) * apply_map(d_mat[1, l], v)
            y_s[0, l] = y1
            y_s[1, l] = y2
            e = y1 - active(0, l) * apply_map(d_mat[0, l], apply_map(u_mat[0, l], y2))
            e_out[l] = e[:1]
        for t in range(4):
            deliver(*msg_e, 4 * i + t)

    @pl.loop(0, wall_count // 2)
    def _(i):
        for t in range(2):
            expect(*msg_b, 2 * i + t)
            expect(*msg_vb, 2 * i + t)
        for t in range(2):
            decode(recv_b, 2 * i + t, t)

    def bwd(i, v):
        d = wall_count - 1 - i
        x_out[d] = v[:1]
        deliver(*msg_x, d)
        expect(*msg_e, d)
        got = got_vec_b[d]
        return apply_coded(d, wide(got[1:2]), v) + wide(e_in[d])

    lax.fori_loop(0, wall_count, bwd, jnp.zeros((8, B), F32))

    @pl.loop(0, lines // 4)
    def _(i):
        for t in range(4):
            expect(*msg_x, 4 * i + t)
        for t in range(4):
            l = 4 * i + t
            v = apply_map(d_mat[1, l], apply_map(u_mat[1, l], wide(x_in[l])))
            x2 = y_s[1, l] - active(1, l) * v
            v = apply_map(d_mat[0, l], apply_map(u_mat[0, l], x2))
            x1 = y_s[0, l] - active(0, l) * v
            out_ref[0, pl.ds(l, 1), :] = x1[:1]
            out_ref[1, pl.ds(l, 1), :] = x2[:1]

    @pl.loop(0, wall_count)
    def _(w):
        @pl.when(w != me)
        def _():
            for msg in (msg_a, msg_va, msg_b, msg_vb, msg_c, msg_e, msg_x):
                post(*msg, w).wait_send()


def per_device(state, source, face_coef, neighbour, lift, elem_slot, line_len, dinv, lower, upper):
    wall = lax.axis_size("wall")
    lines = dinv.shape[1]
    vmem = pl.BlockSpec(memory_space=pltpu.VMEM)
    hbm = pl.BlockSpec(memory_space=pl.ANY)
    raw = pltpu.VMEM((2, 4, B, 8, B), BF)
    mat = pltpu.VMEM((2, lines, B, B), BF)
    coded = pltpu.VMEM((wall, CODED, 128), jnp.int16)
    vec = pltpu.VMEM((wall, 2, B), F32)
    row = pltpu.VMEM((wall, 1, B), F32)
    sems = pltpu.SemaphoreType.DMA((wall,))
    turned = [jnp.transpose(m, (0, 2, 1, 3)) for m in (dinv, lower, upper)]
    return pl.pallas_call(
        kernel,
        out_shape=jax.ShapeDtypeStruct((2, lines, B), F32),
        in_specs=[vmem] * 6 + [pl.BlockSpec(memory_space=pltpu.SMEM)] + [hbm] * 3,
        out_specs=vmem,
        scratch_shapes=[
            raw, raw, raw,
            pltpu.VMEM((4, 2, 8 * B, 128), F32),
            mat, mat, mat,
            pltpu.VMEM((3, 64, B), BF),
            pltpu.VMEM((2, 32, B), F32),
            pltpu.VMEM((2, 168, 128), F32),
            coded, coded, vec, vec, coded, coded, vec, vec,
            pltpu.VMEM((wall, B, B), BF), pltpu.VMEM((wall, B, B), BF),
            pltpu.VMEM((2, lines, 8, B), F32),
            row, row, row, row, row, row,
            pltpu.SemaphoreType.DMA((3, 2, 4)),
            pltpu.SemaphoreType.DMA((2,)), pltpu.SemaphoreType.DMA((2,)),
        ] + [sems] * 14,
        compiler_params=pltpu.CompilerParams(
            collective_id=0, has_side_effects=True, vmem_limit_bytes=67043328
        ),
        name="lines",
    )(state, source, face_coef.T, neighbour.T, lift, elem_slot, line_len, *turned)


def solution(mesh):
    in_specs = (
        P(("wall", "surf"), None),
        P(("wall", "surf"), None),
        P(("wall", "surf"), None),
        P(("wall", "surf"), None),
        P(),
        P("wall", "surf"),
        P("surf"),
        P("wall", "surf", None, None),
        P("wall", "surf", None, None),
        P("wall", "surf", None, None),
    )
    return jax.shard_map(
        per_device, mesh=mesh, in_specs=in_specs, out_specs=P("wall", "surf", None), check_vma=False
    )
```

time: 1470 us -> 133 us (0.09); the launches traced: 1450 us -> 133 us
  waiting for transfers between devices: 958 us -> 0 us
  starting transfers between devices: 411 us -> 0 us
  Pallas kernels: 0 us -> 131 us
  matrix products: 32.2 us -> 0 us
  local copies, waits for them, and re-layouts: 28.4 us -> 1.47 us
    ppermute x64 -> x0, waiting for transfers between devices: 958 us -> none  [the longest x62 958 us: passed_along(): return lax.ppermute(block, axis, route)]
    ppermute x64 -> x0, starting transfers between devices: 411 us -> none  [the longest x62 406 us: passed_along(): return lax.ppermute(block, axis, route)]
    pallas_call x0 -> x1, Pallas kernels: none -> 131 us  [per_device(): pl.pallas_call(kernel, out_shape=jax.ShapeDtypeStruct((2, lines, B), F32)...]
    dot_general x9 -> x0, matrix products: 32.2 us -> none  [the longest x8 32.1 us: apply_block(): jnp.einsum('lij,lj->li', matrix.astype(jnp.float32), vector, precision=la...]
    unnamed x14 -> x1, local copies, waits for them, and re-layouts: 24 us -> 1.47 us
  transfers between devices with their start and end apart: 64 -> 0, of which waited for: 62 -> 0; matrix products, arithmetic and copies ran while one was open for 2% -> 0% of each run, Pallas kernels for 0% -> 0%
where the time goes in v1:
time: 133 us
  Pallas kernels  131 us (98%)
  local copies, waits for them, and re-layouts  1.47 us (1%)
    pallas_call x1, Pallas kernels, per_device(): pl.pallas_call(kernel, out_shape=jax.ShapeDtypeStruct((2, lines, B), F32)...  131 us

profile of v1, /device:TPU:1, one launch (start us, length us, event | category | flops | bytes accessed | tf_op | source)
XLA Modules:
  0.0 132.6 jit_solution(10846266485286993784)
XLA Ops:
  0.0 131.1 %lines.1 = f32[2,32,162]{2,1,0:T(8,128)} custom-call(bf16[64,162]{1,0:T(8,128)(2,1)} %state_ref.1, bf16[64,162]{1,0:T(8,128)(2,1)} %source_ref.1, f32[4,64]{1,0:T(4,128)} %bitcast.8, s32[4,64]{1,0:T(4,128)} %bitcast.9, bf16[162,162]{1,0:T(8,128)(2,1)} %lift_ref.1, s32[2,32]{1,0:T(2,128)} %slot_ref.1, s32[32]{0:T(128)} %len_ref.1, ...), custom_call_target="tpu_custom_call" | custom-call | tf_op jit(solution)/shard_map/lines/pallas_call | solution.py:356
  131.1 1.5 %copy.12 = f32[2,32,162]{2,1,0:T(8,128)} copy(f32[2,32,162]{2,1,0:T(8,128)} %lines.1) | data formatting | bytes 82944

commit v2 on v1

v2 whole, which is shorter than its diff:
```python
import functools

import jax
import jax.numpy as jnp
from jax import lax
from jax.experimental import pallas as pl
from jax.experimental.pallas import tpu as pltpu
from jax.sharding import PartitionSpec as P

MESH = pl.DeviceIdType.MESH
NT = (((1,), (1,)), ((), ()))
TN = (((0,), (0,)), ((), ()))
F32 = jnp.float32
BF = jnp.bfloat16
B = 162
TAIL = B - 128
CHUNK = 56
EARLY = 2
CODED = 168 + CHUNK
TOP = 32512.0
ROUND = 12582912.0


def dot(a, b):
    return jnp.dot(a, b, preferred_element_type=F32)


def halves(m):
    hi = m.astype(BF)
    return hi, (m - hi.astype(F32)).astype(BF)


def product(a, b):
    ah, al = halves(a)
    bh, bl = halves(b)
    return dot(ah, bh) + (dot(ah, bl) + dot(al, bh))


def two_rows(v):
    row = lax.broadcasted_iota(jnp.int32, v.shape, 0)
    hi = v.astype(BF).astype(F32)
    return jnp.where(row % 2 == 0, hi, v - hi).astype(BF)


def apply_map(matrix, v):
    out = lax.dot_general(two_rows(v), matrix, NT, preferred_element_type=F32)
    return out + pltpu.roll(out, 1, 0)


def wide(row):
    return jnp.broadcast_to(row, (8, B))


def kernel(
    state_ref, source_ref, coef_ref, nbr_ref, lift_ref, slot_ref, len_ref, d_hbm, l_hbm, u_hbm,
    out_ref,
    raw, wide_s, d_mat, l_mat, u_mat, ext, rhs, tail_s,
    send_a, recv_a, vec_a, got_vec_a, send_b, recv_b, vec_b, got_vec_b,
    map_h, map_l, y_s, c_out, c_in, e_out, e_in, x_out, x_in,
    load_sem, ext_ss, ext_rs, a_ss, a_rs, va_ss, va_rs, b_ss, b_rs, vb_ss, vb_rs,
    c_ss, c_rs, e_ss, e_rs, x_ss, x_rs,
):
    me = lax.axis_index("wall")
    surf = lax.axis_index("surf")
    wall_count = send_a.shape[0]
    lines = wall_count
    surf_count = lax.axis_size("surf")

    def dev(w):
        return (w, surf)

    hbm = (d_hbm, l_hbm, u_hbm)

    def block(i):
        return lax.rem(i + me // 8, 4)

    def line(b, u):
        return 8 * b + lax.rem(u + me, 8)

    def turn(j):
        return lax.rem(j + me, wall_count)

    def load(k, e, b):
        return pltpu.make_async_copy(
            hbm[k].at[e, :, pl.ds(pl.multiple_of(8 * b, 8), 8), :], raw.at[k, e, b], load_sem.at[k, e, b]
        )

    for ks in ((0, 1), (2,)):
        for i in range(4):
            for k in ks:
                for e in range(2):
                    load(k, e, block(i)).start()

    barrier = pltpu.get_barrier_semaphore()
    after = lax.rem(surf + 1, surf_count)
    before = lax.rem(surf + surf_count - 1, surf_count)
    for s in (after, before):
        pl.semaphore_signal(barrier, inc=1, device_id=(me, s), device_id_type=MESH)

    @pl.loop(0, wall_count)
    def _(w):
        @pl.when(w != me)
        def _():
            pl.semaphore_signal(barrier, inc=1, device_id=dev(w), device_id_type=MESH)

    def active(e, l):
        return jnp.where(2 * me + e < len_ref[l], 1.0, 0.0).astype(F32)

    def widen(k, e, b, slot, first, count):
        v = raw[k, e, b, pl.ds(first, count)].astype(F32)
        rows = pl.ds(pl.multiple_of(first * 8, 8), count * 8)
        wide_s[slot, 0, rows, :] = v[:, :, :128].reshape(count * 8, 128)
        wide_s[slot, 1, rows, pl.ds(0, TAIL)] = v[:, :, 128:].reshape(count * 8, TAIL)

    def one_line(slot, u):
        low = wide_s[slot, 0, pl.ds(u, B, stride=8), :].astype(BF)
        high = wide_s[slot, 1, pl.ds(u, B, stride=8), :]
        return jnp.concatenate([low, high[:, :TAIL].astype(BF)], axis=1)

    def encode(m, keep, store, vec, l, t):
        top = jnp.max(jnp.abs(m), axis=0, keepdims=True)
        inv = jnp.where(top > 0.0, TOP / jnp.where(top > 0.0, top, 1.0), 0.0)
        vec[l, pl.ds(1, 1), :] = top * (keep * (1.0 / TOP))
        q = (m * inv + ROUND) - ROUND
        store[l, pl.ds(0, B), :] = q[:, :128].astype(jnp.int32).astype(jnp.int16)
        tail_s[t, pl.ds(0, B), pl.ds(0, TAIL)] = q[:, 128:]
        packed = tail_s[t, pl.ds(0, CHUNK), :]
        packed = packed + pltpu.roll(tail_s[t, pl.ds(CHUNK, CHUNK), :], 42, 1)
        packed = packed + pltpu.roll(tail_s[t, pl.ds(2 * CHUNK, CHUNK), :], 84, 1)
        store[l, pl.ds(168, CHUNK), :] = packed.astype(jnp.int32).astype(jnp.int16)

    def decode(coded, d, t):
        def split(q):
            v = q.astype(jnp.int32).astype(F32)
            hi = (v * (1.0 / 256.0) + ROUND) - ROUND
            return hi, v - 256.0 * hi

        hi, lo = split(coded[d, pl.ds(0, B), :])
        map_h[d, :, pl.ds(0, 128)] = hi.astype(BF)
        map_l[d, :, pl.ds(0, 128)] = lo.astype(BF)
        packed = coded[d, pl.ds(168, CHUNK), :].astype(jnp.int32).astype(F32)
        for k, shift in ((0, 0), (1, 128 - 42), (2, 128 - 84)):
            part = packed if shift == 0 else pltpu.roll(packed, shift, 1)
            tail_s[t, pl.ds(k * CHUNK, CHUNK), pl.ds(0, TAIL)] = part[:, :TAIL]
        v = tail_s[t, pl.ds(0, B), :][:, :TAIL]
        hi = (v * (1.0 / 256.0) + ROUND) - ROUND
        map_h[d, :, pl.ds(128, TAIL)] = hi.astype(BF)
        map_l[d, :, pl.ds(128, TAIL)] = (v - 256.0 * hi).astype(BF)

    def apply_coded(d, scale, v):
        rows = two_rows(v * scale)
        out = 256.0 * lax.dot_general(rows, map_h[d], NT, preferred_element_type=F32)
        out = out + lax.dot_general(rows, map_l[d], NT, preferred_element_type=F32)
        return out + pltpu.roll(out, 1, 0)

    def post(src, dst, ss, rs, to):
        return pltpu.make_async_remote_copy(
            src_ref=src.at[to], dst_ref=dst.at[me], send_sem=ss.at[to], recv_sem=rs.at[me],
            device_id=dev(to), device_id_type=MESH,
        )

    def arrive(src, dst, ss, rs, frm):
        pltpu.make_async_remote_copy(
            src_ref=src.at[frm], dst_ref=dst.at[frm], send_sem=ss.at[frm], recv_sem=rs.at[frm],
            device_id=dev(frm), device_id_type=MESH,
        ).wait_recv()

    def deliver(src, dst, ss, rs, to):
        @pl.when(to != me)
        def _():
            post(src, dst, ss, rs, to).start()

        @pl.when(to == me)
        def _():
            dst[me] = src[me]

    def expect(src, dst, ss, rs, frm):
        @pl.when(frm != me)
        def _():
            arrive(src, dst, ss, rs, frm)

    msg_a = (send_a, recv_a, a_ss, a_rs)
    msg_va = (vec_a, got_vec_a, va_ss, va_rs)
    msg_b = (send_b, recv_b, b_ss, b_rs)
    msg_vb = (vec_b, got_vec_b, vb_ss, vb_rs)
    msg_c = (c_out, c_in, c_ss, c_rs)
    msg_e = (e_out, e_in, e_ss, e_rs)
    msg_x = (x_out, x_in, x_ss, x_rs)

    tail_s[...] = jnp.zeros_like(tail_s)

    def widen_whole(ks, b, base):
        for n, k in enumerate(ks):
            for e in range(2):
                load(k, e, b).wait()

        @pl.loop(0, 6)
        def _(i):
            for n, k in enumerate(ks):
                for e in range(2):
                    widen(k, e, b, base + 2 * n + e, i * 27, 27)

    def fwd_maps(i, half, send):
        b, after_b = block(i), block(jnp.minimum(i + 1, 3))
        base, other = 4 * lax.rem(i, 2), 4 * lax.rem(i + 1, 2)
        ls = [line(b, 4 * half + t) for t in range(4)]
        for t, l in enumerate(ls):
            u = lax.rem(l, 8)
            m = [one_line(base + s, u) for s in range(4)]
            for e in range(2):
                d_mat[e, l] = m[e]
                l_mat[e, l] = m[2 + e]
            encode(product(dot(m[1], m[3]), dot(m[0], m[2])), active(1, l), send_a, vec_a, l, t)
        for n, k in enumerate((0, 1)):
            for e in range(2):
                widen(k, e, after_b, other + 2 * n + e, half * 81, 81)
        if send:
            for l in ls:
                deliver(*msg_a, l)

    def back_maps(i, half):
        b, after_b = block(i), block(jnp.minimum(i + 1, 3))
        base, other = 4 * lax.rem(i, 2), 4 * lax.rem(i + 1, 2)
        ls = [line(b, 4 * half + t) for t in range(4)]
        for t, l in enumerate(ls):
            u = lax.rem(l, 8)
            m = [one_line(base + s, u) for s in range(2)]
            for e in range(2):
                u_mat[e, l] = m[e]
            both = product(dot(d_mat[0, l], m[0]), dot(d_mat[1, l], m[1]))
            encode(both, active(1, l), send_b, vec_b, l, t)
            vec_b[l, pl.ds(0, 1), :] = jnp.zeros((1, B), F32)
        for e in range(2):
            widen(2, e, after_b, other + e, half * 81, 81)
        for l in ls:
            deliver(*msg_b, l)
            deliver(*msg_vb, l)

    def ready(ks, i):
        @pl.when(i < 3)
        def _():
            for k in ks:
                for e in range(2):
                    load(k, e, block(i + 1)).wait()

    widen_whole((0, 1), block(0), 0)
    ready((0, 1), 0)

    @pl.loop(0, 2)
    def _(half):
        fwd_maps(0, half, False)

    pl.semaphore_wait(barrier, wall_count - 1 + 2)
    halo = []
    for k, (s, place) in enumerate(((after, 0), (before, 2))):
        copy = pltpu.make_async_remote_copy(
            src_ref=state_ref, dst_ref=ext.at[place], send_sem=ext_ss.at[k], recv_sem=ext_rs.at[k],
            device_id=(me, s), device_id_type=MESH,
        )
        copy.start()
        halo.append(copy)
    ext[1] = state_ref[...]

    @pl.loop(0, 8)
    def _(u):
        deliver(*msg_a, line(block(0), u))

    @pl.loop(1, 4)
    def _(i):
        ready((0, 1), i)

        @pl.loop(0, 2)
        def _(half):
            fwd_maps(i, half, True)

    kpos = lax.broadcasted_iota(jnp.int32, (192, 64), 0)
    own = kpos == 64 + lax.broadcasted_iota(jnp.int32, (192, 64), 1)
    weight = jnp.zeros((192, 64), F32)
    for f in range(4):
        hit = kpos == nbr_ref[pl.ds(f, 1), :]
        weight = weight + coef_ref[pl.ds(f, 1), :] * (own.astype(F32) - hit.astype(F32))
    for copy in halo:
        copy.wait()
    w1 = weight.astype(BF)
    rest = weight - w1.astype(F32)
    w2 = rest.astype(BF)
    w3 = (rest - w2.astype(F32)).astype(BF)
    cells = ext[...].reshape(192, B)
    face_sum = sum(
        lax.dot_general(w, cells, TN, preferred_element_type=F32) for w in (w3, w2, w1)
    ).astype(BF)
    spos = lax.broadcasted_iota(jnp.int32, (64, 32), 0)
    for e in range(2):
        pick = (spos == slot_ref[pl.ds(e, 1), :]).astype(F32).astype(BF)
        faces = lax.dot_general(pick, face_sum, TN, preferred_element_type=F32).astype(BF)
        mine = lax.dot_general(pick, source_ref[...], TN, preferred_element_type=F32)
        rhs[e] = mine - dot(faces, lift_ref[...])

    @pl.loop(0, lines // 8)
    def _(i):
        for t in range(8):
            l = turn(8 * i + t)
            y = active(0, l) * apply_map(d_mat[0, l], wide(rhs[0, pl.ds(l, 1), :]))
            y = wide(rhs[1, pl.ds(l, 1), :]) - apply_map(l_mat[1, l], y)
            y = active(1, l) * apply_map(d_mat[1, l], y)
            vec_a[l, pl.ds(0, 1), :] = y[:1]
        for t in range(8):
            deliver(*msg_va, turn(8 * i + t))

    def back_range(lo, hi):
        @pl.loop(lo, hi)
        def _(i):
            ready((2,), i)

            @pl.loop(0, 2)
            def _(half):
                back_maps(i, half)

    widen_whole((2,), block(0), 0)
    back_range(0, EARLY)

    @pl.loop(0, wall_count // 2)
    def _(i):
        for t in range(2):
            expect(*msg_a, 2 * i + t)
            expect(*msg_va, 2 * i + t)
        for t in range(2):
            decode(recv_a, 2 * i + t, t)

    def fwd_step(d, v):
        got = got_vec_a[d]
        return apply_coded(d, wide(got[1:2]), v) + wide(got[0:1])

    def fwd(d, v):
        c_out[d] = v[:1]
        post(*msg_c, d).start()
        return fwd_step(d, v)

    v = lax.fori_loop(0, me, fwd, jnp.zeros((8, B), F32))
    c_in[me] = v[:1]
    lax.fori_loop(me + 1, wall_count, fwd, fwd_step(me, v))

    back_range(EARLY, 4)

    @pl.loop(0, lines // 8)
    def _(i):
        for t in range(8):
            expect(*msg_c, turn(8 * i + t))
        for t in range(8):
            l = turn(8 * i + t)
            v = wide(rhs[0, pl.ds(l, 1), :]) - apply_map(l_mat[0, l], wide(c_in[l]))
            y1 = active(0, l) * apply_map(d_mat[0, l], v)
            v = wide(rhs[1, pl.ds(l, 1), :]) - apply_map(l_mat[1, l], y1)
            y2 = active(1, l) * apply_map(d_mat[1, l], v)
            y_s[0, l] = y1
            y_s[1, l] = y2
            e = y1 - active(0, l) * apply_map(d_mat[0, l], apply_map(u_mat[0, l], y2))
            e_out[l] = e[:1]
        for t in range(8):
            deliver(*msg_e, turn(8 * i + t))

    @pl.loop(0, wall_count // 2)
    def _(i):
        for t in range(2):
            expect(*msg_b, 2 * i + t)
            expect(*msg_vb, 2 * i + t)
        for t in range(2):
            decode(recv_b, 2 * i + t, t)

    def bwd_step(d, v):
        got = got_vec_b[d]
        return apply_coded(d, wide(got[1:2]), v) + wide(e_in[d])

    def bwd(i, v):
        d = wall_count - 1 - i
        x_out[d] = v[:1]
        post(*msg_x, d).start()
        arrive(*msg_e, d)
        return bwd_step(d, v)

    last = wall_count - 1 - me
    v = lax.fori_loop(0, last, bwd, jnp.zeros((8, B), F32))
    x_in[me] = v[:1]
    lax.fori_loop(last + 1, wall_count, bwd, bwd_step(me, v))

    @pl.loop(0, lines // 8)
    def _(i):
        for t in range(8):
            expect(*msg_x, turn(8 * i + t))
        for t in range(8):
            l = turn(8 * i + t)
            v = apply_map(d_mat[1, l], apply_map(u_mat[1, l], wide(x_in[l])))
            x2 = y_s[1, l] - active(1, l) * v
            v = apply_map(d_mat[0, l], apply_map(u_mat[0, l], x2))
            x1 = y_s[0, l] - active(0, l) * v
            out_ref[0, pl.ds(l, 1), :] = x1[:1]
            out_ref[1, pl.ds(l, 1), :] = x2[:1]

    @pl.loop(0, wall_count)
    def _(w):
        @pl.when(w != me)
        def _():
            for msg in (msg_a, msg_va, msg_b, msg_vb, msg_c, msg_e, msg_x):
                post(*msg, w).wait_send()


def per_device(state, source, face_coef, neighbour, lift, elem_slot, line_len, dinv, lower, upper):
    wall = lax.axis_size("wall")
    lines = dinv.shape[1]
    vmem = pl.BlockSpec(memory_space=pltpu.VMEM)
    hbm = pl.BlockSpec(memory_space=pl.ANY)
    raw = pltpu.VMEM((3, 2, 4, B, 8, B), BF)
    mat = pltpu.VMEM((2, lines, B, B), BF)
    coded = pltpu.VMEM((wall, CODED, 128), jnp.int16)
    vec = pltpu.VMEM((wall, 2, B), F32)
    row = pltpu.VMEM((wall, 1, B), F32)
    sems = pltpu.SemaphoreType.DMA((wall,))
    turned = [jnp.transpose(m, (0, 2, 1, 3)) for m in (dinv, lower, upper)]
    return pl.pallas_call(
        kernel,
        out_shape=jax.ShapeDtypeStruct((2, lines, B), F32),
        in_specs=[vmem] * 6 + [pl.BlockSpec(memory_space=pltpu.SMEM)] + [hbm] * 3,
        out_specs=vmem,
        scratch_shapes=[
            raw,
            pltpu.VMEM((8, 2, 8 * B, 128), F32),
            mat, mat, mat,
            pltpu.VMEM((3, 64, B), BF),
            pltpu.VMEM((2, 32, B), F32),
            pltpu.VMEM((4, 168, 128), F32),
            coded, coded, vec, vec, coded, coded, vec, vec,
            pltpu.VMEM((wall, B, B), BF), pltpu.VMEM((wall, B, B), BF),
            pltpu.VMEM((2, lines, 8, B), F32),
            row, row, row, row, row, row,
            pltpu.SemaphoreType.DMA((3, 2, 4)),
            pltpu.SemaphoreType.DMA((2,)), pltpu.SemaphoreType.DMA((2,)),
        ] + [sems] * 14,
        compiler_params=pltpu.CompilerParams(
            collective_id=0, has_side_effects=True, vmem_limit_bytes=67043328
        ),
        name="lines",
    )(state, source, face_coef.T, neighbour.T, lift, elem_slot, line_len, *turned)


def solution(mesh):
    in_specs = (
        P(("wall", "surf"), None),
        P(("wall", "surf"), None),
        P(("wall", "surf"), None),
        P(("wall", "surf"), None),
        P(),
        P("wall", "surf"),
        P("surf"),
        P("wall", "surf", None, None),
        P("wall", "surf", None, None),
        P("wall", "surf", None, None),
    )
    return jax.shard_map(
        per_device, mesh=mesh, in_specs=in_specs, out_specs=P("wall", "surf", None), check_vma=False
    )
```

time: 133 us -> 101 us (0.76)
  Pallas kernels: 131 us -> 99.6 us
    pallas_call x1, Pallas kernels: 131 us -> 99.6 us  [per_device(): pl.pallas_call(kernel, out_shape=jax.ShapeDtypeStruct((2, lines, B), F32)...]
where the time goes in v2:
time: 101 us
  Pallas kernels  99.6 us (99%)
  local copies, waits for them, and re-layouts  1.47 us (1%)
    pallas_call x1, Pallas kernels, per_device(): pl.pallas_call(kernel, out_shape=jax.ShapeDtypeStruct((2, lines, B), F32)...  99.6 us

profile of v2, /device:TPU:1, one launch (start us, length us, event | category | flops | bytes accessed | tf_op | source)
XLA Modules:
  0.0 101.1 jit_solution(3777906479518024421)
XLA Ops:
  0.0 99.6 %lines.1 = f32[2,32,162]{2,1,0:T(8,128)} custom-call(bf16[64,162]{1,0:T(8,128)(2,1)} %state_ref.1, bf16[64,162]{1,0:T(8,128)(2,1)} %source_ref.1, f32[4,64]{1,0:T(4,128)} %bitcast.8, s32[4,64]{1,0:T(4,128)} %bitcast.9, bf16[162,162]{1,0:T(8,128)(2,1)} %lift_ref.1, s32[2,32]{1,0:T(2,128)} %slot_ref.1, s32[32]{0:T(128)} %len_ref.1, ...), custom_call_target="tpu_custom_call" | custom-call | tf_op jit(solution)/shard_map/lines/pallas_call | solution.py:419
  99.6 1.5 %copy.12 = f32[2,32,162]{2,1,0:T(8,128)} copy(f32[2,32,162]{2,1,0:T(8,128)} %lines.1) | data formatting | bytes 82944

commit v3 on v2

v3 whole, which is shorter than its diff:
```python
import functools

import jax
import jax.numpy as jnp
from jax import lax
from jax.experimental import pallas as pl
from jax.experimental.pallas import tpu as pltpu
from jax.sharding import PartitionSpec as P

MESH = pl.DeviceIdType.MESH
NT = (((1,), (1,)), ((), ()))
TN = (((0,), (0,)), ((), ()))
F32 = jnp.float32
BF = jnp.bfloat16
B = 162
TAIL = B - 128
CHUNK = 56
FIRST = 8
CODED = 168 + CHUNK
TOP = 32512.0
ROUND = 12582912.0


def dot(a, b):
    return jnp.dot(a, b, preferred_element_type=F32)


def halves(m):
    hi = m.astype(BF)
    return hi, (m - hi.astype(F32)).astype(BF)


def product(a, b):
    ah, al = halves(a)
    bh, bl = halves(b)
    return dot(ah, bh) + (dot(ah, bl) + dot(al, bh))


def two_rows(v):
    row = lax.broadcasted_iota(jnp.int32, v.shape, 0)
    hi = v.astype(BF).astype(F32)
    return jnp.where(row % 2 == 0, hi, v - hi).astype(BF)


def apply_map(matrix, v):
    out = lax.dot_general(two_rows(v), matrix, NT, preferred_element_type=F32)
    return out + pltpu.roll(out, 1, 0)


def wide(row):
    return jnp.broadcast_to(row, (8, B))


def kernel(
    state_ref, source_ref, coef_ref, nbr_ref, lift_ref, slot_ref, len_ref, d_hbm, l_hbm, u_hbm,
    out_ref,
    raw, perm, last, prod, t_hi, t_lo, d_mat, l_mat, u_mat, ext, rhs, tail_s,
    send_a, recv_a, vec_a, got_vec_a, send_b, recv_b, vec_b, got_vec_b,
    map_h, map_l, y_s, c_out, c_in, e_out, e_in, x_out, x_in,
    load_sem, ext_ss, ext_rs, a_ss, a_rs, va_ss, va_rs, b_ss, b_rs, vb_ss, vb_rs,
    c_ss, c_rs, e_ss, e_rs, x_ss, x_rs,
):
    me = lax.axis_index("wall")
    surf = lax.axis_index("surf")
    wall_count = send_a.shape[0]
    lines = wall_count
    surf_count = lax.axis_size("surf")

    def dev(w):
        return (w, surf)

    hbm = (d_hbm, l_hbm, u_hbm)

    my_y, my_x, my_c = me // 8, lax.rem(me // 2, 4), lax.rem(me, 2)
    my_b, my_u = lax.rem(my_x + my_y, 4), 2 * my_y + my_c
    mine = 8 * my_b + my_u

    def block(i):
        return lax.rem(i + my_b, 4)

    def line(b, u):
        return 8 * b + lax.rem(u + my_u, 8)

    def owner(l):
        y = lax.rem(l, 8) // 2
        return 8 * y + 2 * lax.rem(l // 8 - y + 4, 4) + lax.rem(l, 2)

    def turn(j):
        return line(block(j // 8), lax.rem(j, 8))

    def away(j):
        return lax.rem(j + me, wall_count)

    def load(k, e, b):
        return pltpu.make_async_copy(
            hbm[k].at[e, :, pl.ds(pl.multiple_of(8 * b, 8), 8), :], raw.at[k, e, b], load_sem.at[k, e, b]
        )

    for ks in ((0, 1), (2,)):
        for i in range(4):
            for k in ks:
                for e in range(2):
                    load(k, e, block(i)).start()

    barrier = pltpu.get_barrier_semaphore()
    after = lax.rem(surf + 1, surf_count)
    before = lax.rem(surf + surf_count - 1, surf_count)
    for s in (after, before):
        pl.semaphore_signal(barrier, inc=1, device_id=(me, s), device_id_type=MESH)

    @pl.loop(0, wall_count)
    def _(w):
        @pl.when(w != me)
        def _():
            pl.semaphore_signal(barrier, inc=1, device_id=dev(w), device_id_type=MESH)

    def active(e, l):
        return jnp.where(2 * me + e < len_ref[l], 1.0, 0.0).astype(F32)

    def encode(m, keep, store, vec, l, t):
        top = jnp.max(jnp.abs(m), axis=0, keepdims=True)
        inv = jnp.where(top > 0.0, TOP / jnp.where(top > 0.0, top, 1.0), 0.0)
        vec[l, pl.ds(1, 1), :] = top * (keep * (1.0 / TOP))
        q = (m * inv + ROUND) - ROUND
        store[l, pl.ds(0, B), :] = q[:, :128].astype(jnp.int32).astype(jnp.int16)
        tail_s[t, pl.ds(0, B), pl.ds(0, TAIL)] = q[:, 128:]
        packed = tail_s[t, pl.ds(0, CHUNK), :]
        packed = packed + pltpu.roll(tail_s[t, pl.ds(CHUNK, CHUNK), :], 42, 1)
        packed = packed + pltpu.roll(tail_s[t, pl.ds(2 * CHUNK, CHUNK), :], 84, 1)
        store[l, pl.ds(168, CHUNK), :] = packed.astype(jnp.int32).astype(jnp.int16)

    def decode(coded, d, t):
        def split(q):
            v = q.astype(jnp.int32).astype(F32)
            hi = (v * (1.0 / 256.0) + ROUND) - ROUND
            return hi, v - 256.0 * hi

        hi, lo = split(coded[d, pl.ds(0, B), :])
        map_h[d, :, pl.ds(0, 128)] = hi.astype(BF)
        map_l[d, :, pl.ds(0, 128)] = lo.astype(BF)
        packed = coded[d, pl.ds(168, CHUNK), :].astype(jnp.int32).astype(F32)
        for k, shift in ((0, 0), (1, 128 - 42), (2, 128 - 84)):
            part = packed if shift == 0 else pltpu.roll(packed, shift, 1)
            tail_s[t, pl.ds(k * CHUNK, CHUNK), pl.ds(0, TAIL)] = part[:, :TAIL]
        v = tail_s[t, pl.ds(0, B), :][:, :TAIL]
        hi = (v * (1.0 / 256.0) + ROUND) - ROUND
        map_h[d, :, pl.ds(128, TAIL)] = hi.astype(BF)
        map_l[d, :, pl.ds(128, TAIL)] = (v - 256.0 * hi).astype(BF)

    def apply_coded(d, scale, v):
        rows = two_rows(v * scale)
        out = 256.0 * lax.dot_general(rows, map_h[d], NT, preferred_element_type=F32)
        out = out + lax.dot_general(rows, map_l[d], NT, preferred_element_type=F32)
        return out + pltpu.roll(out, 1, 0)

    def copy_of(src, dst, ss, rs, slot, place, to):
        return pltpu.make_async_remote_copy(
            src_ref=src.at[slot], dst_ref=dst.at[place], send_sem=ss,
            recv_sem=rs.at[place] if rs.shape else rs, device_id=dev(to), device_id_type=MESH,
        )

    def to_owner(msg, l):
        copy_of(*msg, l, me, owner(l)).start()

    def to_device(msg, d):
        copy_of(*msg, d, mine, d).start()

    def arrive(msg, frm):
        copy_of(*msg, frm, frm, frm).wait_recv()

    def everyone(src, dst, ss, rs):
        part = pl.ds(0, wall_count - 1)
        return pltpu.make_async_remote_copy(
            src_ref=src.at[part], dst_ref=dst.at[part], send_sem=ss,
            recv_sem=rs.at[0] if rs.shape else rs, device_id=dev(away(1)), device_id_type=MESH,
        )

    def send_turns(msg, lo, hi):
        @pl.loop(lo, hi)
        def _(j):
            to_owner(msg, turn(j))

    msg_a = (send_a, recv_a, a_ss, a_rs)
    msg_va = (vec_a, got_vec_a, va_ss, va_rs)
    msg_b = (send_b, recv_b, b_ss, b_rs)
    msg_vb = (vec_b, got_vec_b, vb_ss, vb_rs)
    msg_c = (c_out, c_in, c_ss, c_rs)
    msg_e = (e_out, e_in, e_ss, e_rs)
    msg_x = (x_out, x_in, x_ss, x_rs)

    tail_s[...] = jnp.zeros_like(tail_s)
    row = lax.broadcasted_iota(jnp.int32, (128, 128), 0)
    col = lax.broadcasted_iota(jnp.int32, (128, 128), 1)
    perm[...] = (col == 8 * lax.rem(row, 16) + row // 16).astype(F32).astype(BF)
    row = lax.broadcasted_iota(jnp.int32, (64, 16), 0)
    col = lax.broadcasted_iota(jnp.int32, (64, 16), 1)
    last[...] = (col == 8 * lax.rem(row, 8) + row // 8).astype(F32).astype(BF)

    def stored_product(t, a, b):
        return dot(t_hi[t, a], t_hi[t, b]) + (dot(t_hi[t, a], t_lo[t, b]) + dot(t_lo[t, a], t_hi[t, b]))

    def gather_lines(sources, b):
        for k, store in sources:
            for e in range(2):
                load(k, e, b).wait()

        @pl.loop(0, 2)
        def _(c):
            for t in range(5):
                first = pl.multiple_of(80 * c + 16 * t, 16)
                for k, store in sources:
                    for e in range(2):
                        x = raw[k, e, b, pl.ds(first, 16)].reshape(128, B)
                        y = dot(perm[...], x).astype(BF)
                        for u in range(8):
                            store[e, 8 * b + u, pl.ds(first, 16), :] = y[16 * u : 16 * u + 16]

        for k, store in sources:
            for e in range(2):
                x = raw[k, e, b, pl.ds(160, 2)].reshape(16, B)
                y = dot(last[...], x).astype(BF)
                for u in range(8):
                    store[e, 8 * b + u, pl.ds(160, 2), :] = y[8 * u : 8 * u + 2]

    def steps(b, right):
        for u in range(8):
            for e in range(2):
                t_hi[u, e], t_lo[u, e] = halves(dot(d_mat[e, 8 * b + u], right[e, 8 * b + u]))

    def fwd_maps(i, send):
        b = block(i)
        gather_lines(((0, d_mat), (1, l_mat)), b)
        steps(b, l_mat)

        for t in range(8):
            prod[t] = stored_product(t, 1, 0)
        for t in range(8):
            encode(prod[t], active(1, 8 * b + t), send_a, vec_a, 8 * b + t, t % 4)

        if send:
            @pl.loop(0, 8)
            def _(u):
                to_owner(msg_a, line(b, u))

    def back_maps(i):
        b = block(i)
        gather_lines(((2, u_mat),), b)
        steps(b, u_mat)

        for t in range(8):
            prod[t] = stored_product(t, 0, 1)
        for t in range(8):
            l = 8 * b + t
            encode(prod[t], active(1, l), send_b, vec_b, l, t % 4)
            vec_b[l, pl.ds(0, 1), :] = jnp.zeros((1, B), F32)

    fwd_maps(0, False)

    pl.semaphore_wait(barrier, wall_count - 1 + 2)
    halo = []
    for k, (s, place) in enumerate(((after, 0), (before, 2))):
        copy = pltpu.make_async_remote_copy(
            src_ref=state_ref, dst_ref=ext.at[place], send_sem=ext_ss.at[k], recv_sem=ext_rs.at[k],
            device_id=(me, s), device_id_type=MESH,
        )
        copy.start()
        halo.append(copy)
    ext[1] = state_ref[...]

    @pl.loop(1, 8)
    def _(u):
        to_owner(msg_a, line(block(0), u))

    recv_a[me] = send_a[mine]

    @pl.loop(1, 4)
    def _(i):
        fwd_maps(i, True)

    kpos = lax.broadcasted_iota(jnp.int32, (192, 64), 0)
    own = kpos == 64 + lax.broadcasted_iota(jnp.int32, (192, 64), 1)
    weight = jnp.zeros((192, 64), F32)
    for f in range(4):
        hit = kpos == nbr_ref[pl.ds(f, 1), :]
        weight = weight + coef_ref[pl.ds(f, 1), :] * (own.astype(F32) - hit.astype(F32))
    for copy in halo:
        copy.wait()
    w1 = weight.astype(BF)
    rest = weight - w1.astype(F32)
    w2 = rest.astype(BF)
    w3 = (rest - w2.astype(F32)).astype(BF)
    cells = ext[...].reshape(192, B)
    face_sum = sum(
        lax.dot_general(w, cells, TN, preferred_element_type=F32) for w in (w3, w2, w1)
    ).astype(BF)
    spos = lax.broadcasted_iota(jnp.int32, (64, 32), 0)
    for e in range(2):
        pick = (spos == slot_ref[pl.ds(e, 1), :]).astype(F32).astype(BF)
        faces = lax.dot_general(pick, face_sum, TN, preferred_element_type=F32).astype(BF)
        own_rows = lax.dot_general(pick, source_ref[...], TN, preferred_element_type=F32)
        rhs[e] = own_rows - dot(faces, lift_ref[...])

    @pl.loop(0, lines // 8)
    def _(i):
        ls = [turn(8 * i + t) for t in range(8)]
        y = [active(0, l) * apply_map(d_mat[0, l], wide(rhs[0, pl.ds(l, 1), :])) for l in ls]
        y = [wide(rhs[1, pl.ds(l, 1), :]) - apply_map(l_mat[1, l], v) for l, v in zip(ls, y)]
        y = [active(1, l) * apply_map(d_mat[1, l], v) for l, v in zip(ls, y)]
        for l, v in zip(ls, y):
            vec_a[l, pl.ds(0, 1), :] = v[:1]
        send_turns(msg_va, jnp.maximum(8 * i, 1), 8 * i + 8)

    got_vec_a[me] = vec_a[mine]

    def sender(j):
        return owner(8 * lax.rem(my_b - j // 8 + 4, 4) + lax.rem(my_u - j + 32, 8))

    def take(msg, i):
        @pl.loop(0, 4)
        def _(q):
            js = [8 * i + 2 * q + t for t in range(2)]
            for j in js:
                @pl.when(j > 0)
                def _():
                    arrive(msg, sender(j))
            for t, j in enumerate(js):
                decode(msg[1], sender(j), t)

    def send_back(lo, hi):
        @pl.loop(lo, hi)
        def _(j):
            to_owner(msg_b, turn(j))
            to_owner(msg_vb, turn(j))

    @pl.loop(0, 4)
    def _(i):
        back_maps(i)
        send_back(1, jnp.where(i == 0, FIRST, 1))
        take(msg_a, i)

    everyone(*msg_va).wait_recv()

    def send_four(msg, i):
        for t in range(4):
            @pl.when(4 * i + t != me)
            def _():
                to_device(msg, 4 * i + t)

    def fwd(i, v):
        for t in range(4):
            d = 4 * i + t
            c_out[d] = v[:1]
            got = got_vec_a[d]
            v = apply_coded(d, wide(got[1:2]), v) + wide(got[0:1])
        send_four(msg_c, i)
        return v

    lax.fori_loop(0, wall_count // 4, fwd, jnp.zeros((8, B), F32))
    c_in[mine] = c_out[me]

    send_back(FIRST, wall_count)

    everyone(*msg_c).wait_recv()

    @pl.loop(0, lines // 8)
    def _(i):
        ls = [turn(8 * i + t) for t in range(8)]
        v = [wide(rhs[0, pl.ds(l, 1), :]) - apply_map(l_mat[0, l], wide(c_in[l])) for l in ls]
        first = [active(0, l) * apply_map(d_mat[0, l], v) for l, v in zip(ls, v)]
        for l, y in zip(ls, first):
            y_s[0, l] = y
        v = [wide(rhs[1, pl.ds(l, 1), :]) - apply_map(l_mat[1, l], y) for l, y in zip(ls, first)]
        second = [active(1, l) * apply_map(d_mat[1, l], v) for l, v in zip(ls, v)]
        for l, y in zip(ls, second):
            y_s[1, l] = y
        v = [apply_map(u_mat[0, l], y) for l, y in zip(ls, second)]
        v = [active(0, l) * apply_map(d_mat[0, l], v) for l, v in zip(ls, v)]
        for l, y, e in zip(ls, first, v):
            e_out[l] = y[:1] - e[:1]
        send_turns(msg_e, jnp.maximum(8 * i, 1), 8 * i + 8)

    e_in[me] = e_out[mine]

    recv_b[me] = send_b[mine]
    got_vec_b[me] = vec_b[mine]

    @pl.loop(0, 4)
    def _(i):
        take(msg_b, i)

    everyone(*msg_vb).wait_recv()
    everyone(*msg_e).wait_recv()

    def bwd(k, v):
        i = wall_count // 4 - 1 - k
        for t in reversed(range(4)):
            d = 4 * i + t
            x_out[d] = v[:1]
            got = got_vec_b[d]
            v = apply_coded(d, wide(got[1:2]), v) + wide(e_in[d])
        send_four(msg_x, i)
        return v

    lax.fori_loop(0, wall_count // 4, bwd, jnp.zeros((8, B), F32))
    x_in[mine] = x_out[me]

    everyone(*msg_x).wait_recv()

    @pl.loop(0, lines // 8)
    def _(i):
        ls = [turn(8 * i + t) for t in range(8)]
        v = [apply_map(u_mat[1, l], wide(x_in[l])) for l in ls]
        v = [apply_map(d_mat[1, l], v) for l, v in zip(ls, v)]
        x = [y_s[1, l] - active(1, l) * v for l, v in zip(ls, v)]
        for l, v in zip(ls, x):
            out_ref[1, pl.ds(l, 1), :] = v[:1]
        v = [apply_map(u_mat[0, l], v) for l, v in zip(ls, x)]
        v = [apply_map(d_mat[0, l], v) for l, v in zip(ls, v)]
        for l, v in zip(ls, v):
            out_ref[0, pl.ds(l, 1), :] = y_s[0, l][:1] - active(0, l) * v[:1]

    for msg in (msg_a, msg_va, msg_b, msg_vb, msg_c, msg_e, msg_x):
        everyone(*msg).wait_send()


def per_device(state, source, face_coef, neighbour, lift, elem_slot, line_len, dinv, lower, upper):
    wall = lax.axis_size("wall")
    lines = dinv.shape[1]
    vmem = pl.BlockSpec(memory_space=pltpu.VMEM)
    hbm = pl.BlockSpec(memory_space=pl.ANY)
    raw = pltpu.VMEM((3, 2, 4, B, 8, B), BF)
    mat = pltpu.VMEM((2, lines, B, B), BF)
    coded = pltpu.VMEM((wall, CODED, 128), jnp.int16)
    vec = pltpu.VMEM((wall, 2, B), F32)
    row = pltpu.VMEM((wall, 1, B), F32)
    sems = pltpu.SemaphoreType.DMA((wall,))
    one = pltpu.SemaphoreType.DMA
    turned = [jnp.transpose(m, (0, 2, 1, 3)) for m in (dinv, lower, upper)]
    return pl.pallas_call(
        kernel,
        out_shape=jax.ShapeDtypeStruct((2, lines, B), F32),
        in_specs=[vmem] * 6 + [pl.BlockSpec(memory_space=pltpu.SMEM)] + [hbm] * 3,
        out_specs=vmem,
        scratch_shapes=[
            raw,
            pltpu.VMEM((128, 128), BF), pltpu.VMEM((64, 16), BF),
            pltpu.VMEM((8, B, B), F32),
            pltpu.VMEM((8, 2, B, B), BF), pltpu.VMEM((8, 2, B, B), BF),
            mat, mat, mat,
            pltpu.VMEM((3, 64, B), BF),
            pltpu.VMEM((2, 32, B), F32),
            pltpu.VMEM((4, 168, 128), F32),
            coded, coded, vec, vec, coded, coded, vec, vec,
            pltpu.VMEM((wall, B, B), BF), pltpu.VMEM((wall, B, B), BF),
            pltpu.VMEM((2, lines, 8, B), F32),
            row, row, row, row, row, row,
            pltpu.SemaphoreType.DMA((3, 2, 4)),
            pltpu.SemaphoreType.DMA((2,)), pltpu.SemaphoreType.DMA((2,)),
        ] + [one, sems, one, one, one, sems] + [one] * 8,
        compiler_params=pltpu.CompilerParams(
            collective_id=0, has_side_effects=True, vmem_limit_bytes=67043328
        ),
        name="lines",
    )(state, source, face_coef.T, neighbour.T, lift, elem_slot, line_len, *turned)


def solution(mesh):
    in_specs = (
        P(("wall", "surf"), None),
        P(("wall", "surf"), None),
        P(("wall", "surf"), None),
        P(("wall", "surf"), None),
        P(),
        P("wall", "surf"),
        P("surf"),
        P("wall", "surf", None, None),
        P("wall", "surf", None, None),
        P("wall", "surf", None, None),
    )
    return jax.shard_map(
        per_device, mesh=mesh, in_specs=in_specs, out_specs=P("wall", "surf", None), check_vma=False
    )
```

time: 101 us -> 76.5 us (0.76)
  Pallas kernels: 99.6 us -> 74.8 us
    pallas_call x1, Pallas kernels: 99.6 us -> 74.8 us  [per_device(): pl.pallas_call(kernel, out_shape=jax.ShapeDtypeStruct((2, lines, B), F32)...]
where the time goes in v3:
time: 76.5 us; the launch traced here: 76.3 us
  Pallas kernels  74.8 us (98%)
  local copies, waits for them, and re-layouts  1.47 us (2%)
    pallas_call x1, Pallas kernels, per_device(): pl.pallas_call(kernel, out_shape=jax.ShapeDtypeStruct((2, lines, B), F32)...  74.8 us

profile of v3, /device:TPU:1, one launch (start us, length us, event | category | flops | bytes accessed | tf_op | source)
XLA Modules:
  0.0 76.3 jit_solution(3152955579365823534)
XLA Ops:
  0.0 74.8 %lines.1 = f32[2,32,162]{2,1,0:T(8,128)} custom-call(bf16[64,162]{1,0:T(8,128)(2,1)} %state_ref.1, bf16[64,162]{1,0:T(8,128)(2,1)} %source_ref.1, f32[4,64]{1,0:T(4,128)} %bitcast.8, s32[4,64]{1,0:T(4,128)} %bitcast.9, bf16[162,162]{1,0:T(8,128)(2,1)} %lift_ref.1, s32[2,32]{1,0:T(2,128)} %slot_ref.1, s32[32]{0:T(128)} %len_ref.1, ...), custom_call_target="tpu_custom_call" | custom-call | tf_op jit(solution)/shard_map/lines/pallas_call | solution.py:439
  74.8 1.5 %copy.12 = f32[2,32,162]{2,1,0:T(8,128)} copy(f32[2,32,162]{2,1,0:T(8,128)} %lines.1) | data formatting | bytes 82944

commit v4 on v3

--- a/solution.py
+++ b/solution.py
@@ -15,7 +15,7 @@
 B = 162
 TAIL = B - 128
 CHUNK = 56
-FIRST = 8
+FIRST = 16
 CODED = 168 + CHUNK
 TOP = 32512.0
 ROUND = 12582912.0
@@ -52,12 +52,13 @@
 
 
 def kernel(
-    state_ref, source_ref, coef_ref, nbr_ref, lift_ref, slot_ref, len_ref, d_hbm, l_hbm, u_hbm,
+    state_hbm, source_hbm, coef_hbm, nbr_hbm, lift_hbm, slot_hbm, len_ref, d_hbm, l_hbm, u_hbm,
     out_ref,
+    source_ref, coef_ref, nbr_ref, lift_ref, slot_ref, v_mat, b_mat,
     raw, perm, last, prod, t_hi, t_lo, d_mat, l_mat, u_mat, ext, rhs, tail_s,
     send_a, recv_a, vec_a, got_vec_a, send_b, recv_b, vec_b, got_vec_b,
     map_h, map_l, y_s, c_out, c_in, e_out, e_in, x_out, x_in,
-    load_sem, ext_ss, ext_rs, a_ss, a_rs, va_ss, va_rs, b_ss, b_rs, vb_ss, vb_rs,
+    small_sem, load_sem, ext_ss, ext_rs, a_ss, a_rs, va_ss, va_rs, b_ss, b_rs, vb_ss, vb_rs,
     c_ss, c_rs, e_ss, e_rs, x_ss, x_rs,
 ):
     me = lax.axis_index("wall")
@@ -96,11 +97,9 @@
             hbm[k].at[e, :, pl.ds(pl.multiple_of(8 * b, 8), 8), :], raw.at[k, e, b], load_sem.at[k, e, b]
         )
 
-    for ks in ((0, 1), (2,)):
-        for i in range(4):
-            for k in ks:
-                for e in range(2):
-                    load(k, e, block(i)).start()
+    for k in range(2):
+        for e in range(2):
+            load(k, e, block(0)).start()
 
     barrier = pltpu.get_barrier_semaphore()
     after = lax.rem(surf + 1, surf_count)
@@ -118,8 +117,8 @@
         return jnp.where(2 * me + e < len_ref[l], 1.0, 0.0).astype(F32)
 
     def encode(m, keep, store, vec, l, t):
-        top = jnp.max(jnp.abs(m), axis=0, keepdims=True)
-        inv = jnp.where(top > 0.0, TOP / jnp.where(top > 0.0, top, 1.0), 0.0)
+        top = jnp.maximum(jnp.max(jnp.abs(m), axis=0, keepdims=True), 1e-30)
+        inv = TOP / top
         vec[l, pl.ds(1, 1), :] = top * (keep * (1.0 / TOP))
         q = (m * inv + ROUND) - ROUND
         store[l, pl.ds(0, B), :] = q[:, :128].astype(jnp.int32).astype(jnp.int16)
@@ -188,6 +187,21 @@
     msg_e = (e_out, e_in, e_ss, e_rs)
     msg_x = (x_out, x_in, x_ss, x_rs)
 
+    small = [
+        pltpu.make_async_copy(src, dst, small_sem.at[n])
+        for n, (src, dst) in enumerate((
+            (state_hbm, ext.at[1]), (source_hbm, source_ref), (coef_hbm, coef_ref),
+            (nbr_hbm, nbr_ref), (lift_hbm, lift_ref), (slot_hbm, slot_ref),
+        ))
+    ]
+    for copy in small:
+        copy.start()
+    for ks, first in (((0, 1), 1), ((2,), 0)):
+        for n in range(first, 4):
+            for k in ks:
+                for e in range(2):
+                    load(k, e, block(n)).start()
+
     tail_s[...] = jnp.zeros_like(tail_s)
     row = lax.broadcasted_iota(jnp.int32, (128, 128), 0)
     col = lax.broadcasted_iota(jnp.int32, (128, 128), 1)
@@ -251,21 +265,24 @@
             prod[t] = stored_product(t, 0, 1)
         for t in range(8):
             l = 8 * b + t
+            v_mat[l] = t_hi[t, 1]
+            b_mat[l] = prod[t].astype(BF)
             encode(prod[t], active(1, l), send_b, vec_b, l, t % 4)
             vec_b[l, pl.ds(0, 1), :] = jnp.zeros((1, B), F32)
 
     fwd_maps(0, False)
 
+    for copy in small:
+        copy.wait()
     pl.semaphore_wait(barrier, wall_count - 1 + 2)
     halo = []
     for k, (s, place) in enumerate(((after, 0), (before, 2))):
         copy = pltpu.make_async_remote_copy(
-            src_ref=state_ref, dst_ref=ext.at[place], send_sem=ext_ss.at[k], recv_sem=ext_rs.at[k],
+            src_ref=ext.at[1], dst_ref=ext.at[place], send_sem=ext_ss.at[k], recv_sem=ext_rs.at[k],
             device_id=(me, s), device_id_type=MESH,
         )
         copy.start()
         halo.append(copy)
-    ext[1] = state_ref[...]
 
     @pl.loop(1, 8)
     def _(u):
@@ -335,7 +352,7 @@
     @pl.loop(0, 4)
     def _(i):
         back_maps(i)
-        send_back(1, jnp.where(i == 0, FIRST, 1))
+        send_back(jnp.maximum(8 * i, 1), jnp.minimum(8 * i + 8, FIRST))
         take(msg_a, i)
 
     everyone(*msg_va).wait_recv()
@@ -367,8 +384,6 @@
         ls = [turn(8 * i + t) for t in range(8)]
         v = [wide(rhs[0, pl.ds(l, 1), :]) - apply_map(l_mat[0, l], wide(c_in[l])) for l in ls]
         first = [active(0, l) * apply_map(d_mat[0, l], v) for l, v in zip(ls, v)]
-        for l, y in zip(ls, first):
-            y_s[0, l] = y
         v = [wide(rhs[1, pl.ds(l, 1), :]) - apply_map(l_mat[1, l], y) for l, y in zip(ls, first)]
         second = [active(1, l) * apply_map(d_mat[1, l], v) for l, v in zip(ls, v)]
         for l, y in zip(ls, second):
@@ -409,15 +424,11 @@
     @pl.loop(0, lines // 8)
     def _(i):
         ls = [turn(8 * i + t) for t in range(8)]
-        v = [apply_map(u_mat[1, l], wide(x_in[l])) for l in ls]
-        v = [apply_map(d_mat[1, l], v) for l, v in zip(ls, v)]
-        x = [y_s[1, l] - active(1, l) * v for l, v in zip(ls, v)]
-        for l, v in zip(ls, x):
-            out_ref[1, pl.ds(l, 1), :] = v[:1]
-        v = [apply_map(u_mat[0, l], v) for l, v in zip(ls, x)]
-        v = [apply_map(d_mat[0, l], v) for l, v in zip(ls, v)]
-        for l, v in zip(ls, v):
-            out_ref[0, pl.ds(l, 1), :] = y_s[0, l][:1] - active(0, l) * v[:1]
+        v = [apply_map(v_mat[l], wide(x_in[l])) for l in ls]
+        w = [apply_map(b_mat[l], wide(x_in[l])) for l in ls]
+        for l, v, w in zip(ls, v, w):
+            out_ref[1, pl.ds(l, 1), :] = y_s[1, l][:1] - active(1, l) * v[:1]
+            out_ref[0, pl.ds(l, 1), :] = e_out[l] + active(1, l) * w[:1]
 
     for msg in (msg_a, msg_va, msg_b, msg_vb, msg_c, msg_e, msg_x):
         everyone(*msg).wait_send()
@@ -439,9 +450,12 @@
     return pl.pallas_call(
         kernel,
         out_shape=jax.ShapeDtypeStruct((2, lines, B), F32),
-        in_specs=[vmem] * 6 + [pl.BlockSpec(memory_space=pltpu.SMEM)] + [hbm] * 3,
+        in_specs=[hbm] * 6 + [pl.BlockSpec(memory_space=pltpu.SMEM)] + [hbm] * 3,
         out_specs=vmem,
         scratch_shapes=[
+            pltpu.VMEM((64, B), BF), pltpu.VMEM((4, 64), F32), pltpu.VMEM((4, 64), jnp.int32),
+            pltpu.VMEM((B, B), BF), pltpu.VMEM((2, lines), jnp.int32),
+            pltpu.VMEM((lines, B, B), BF), pltpu.VMEM((lines, B, B), BF),
             raw,
             pltpu.VMEM((128, 128), BF), pltpu.VMEM((64, 16), BF),
             pltpu.VMEM((8, B, B), F32),
@@ -454,6 +468,7 @@
             pltpu.VMEM((wall, B, B), BF), pltpu.VMEM((wall, B, B), BF),
             pltpu.VMEM((2, lines, 8, B), F32),
             row, row, row, row, row, row,
+            pltpu.SemaphoreType.DMA((6,)),
             pltpu.SemaphoreType.DMA((3, 2, 4)),
             pltpu.SemaphoreType.DMA((2,)), pltpu.SemaphoreType.DMA((2,)),
         ] + [one, sems, one, one, one, sems] + [one] * 8,

time: 76.5 us -> 74.5 us (0.974)
  Pallas kernels: 74.8 us -> 72.8 us
    pallas_call x1, Pallas kernels: 74.8 us -> 72.8 us  [per_device(): pl.pallas_call(kernel, out_shape=jax.ShapeDtypeStruct((2, lines, B), F32)...]
where the time goes in v4:
time: 74.5 us; the launch traced here: 74.3 us
  Pallas kernels  72.8 us (98%)
  local copies, waits for them, and re-layouts  1.47 us (2%)
    pallas_call x1, Pallas kernels, per_device(): pl.pallas_call(kernel, out_shape=jax.ShapeDtypeStruct((2, lines, B), F32)...  72.8 us

profile of v4, /device:TPU:1, one launch (start us, length us, event | category | flops | bytes accessed | tf_op | source)
XLA Modules:
  0.0 74.3 jit_solution(4661828444497846200)
XLA Ops:
  0.0 72.8 %lines.1 = f32[2,32,162]{2,1,0:T(8,128)} custom-call(bf16[64,162]{1,0:T(8,128)(2,1)} %state_hbm.1, bf16[64,162]{1,0:T(8,128)(2,1)} %source_hbm.1, f32[4,64]{1,0:T(4,128)} %bitcast.8, s32[4,64]{1,0:T(4,128)} %bitcast.9, bf16[162,162]{1,0:T(8,128)(2,1)} %lift_hbm.1, s32[2,32]{1,0:T(2,128)} %slot_hbm.1, s32[32]{0:T(128)} %len_ref.1, ...), custom_call_target="tpu_custom_call" | custom-call | tf_op jit(solution)/shard_map/lines/pallas_call | solution.py:450
  72.9 1.5 %copy.12 = f32[2,32,162]{2,1,0:T(8,128)} copy(f32[2,32,162]{2,1,0:T(8,128)} %lines.1) | data formatting | bytes 82944

commit v5 on v4

--- a/solution.py
+++ b/solution.py
@@ -357,22 +357,22 @@
 
     everyone(*msg_va).wait_recv()
 
-    def send_four(msg, i):
-        for t in range(4):
-            @pl.when(4 * i + t != me)
+    def send_group(msg, i):
+        for t in range(8):
+            @pl.when(8 * i + t != me)
             def _():
-                to_device(msg, 4 * i + t)
+                to_device(msg, 8 * i + t)
 
     def fwd(i, v):
-        for t in range(4):
-            d = 4 * i + t
+        for t in range(8):
+            d = 8 * i + t
             c_out[d] = v[:1]
             got = got_vec_a[d]
             v = apply_coded(d, wide(got[1:2]), v) + wide(got[0:1])
-        send_four(msg_c, i)
+        send_group(msg_c, i)
         return v
 
-    lax.fori_loop(0, wall_count // 4, fwd, jnp.zeros((8, B), F32))
+    lax.fori_loop(0, wall_count // 8, fwd, jnp.zeros((8, B), F32))
     c_in[mine] = c_out[me]
 
     send_back(FIRST, wall_count)
@@ -407,16 +407,16 @@
     everyone(*msg_e).wait_recv()
 
     def bwd(k, v):
-        i = wall_count // 4 - 1 - k
-        for t in reversed(range(4)):
-            d = 4 * i + t
+        i = wall_count // 8 - 1 - k
+        for t in reversed(range(8)):
+            d = 8 * i + t
             x_out[d] = v[:1]
             got = got_vec_b[d]
             v = apply_coded(d, wide(got[1:2]), v) + wide(e_in[d])
-        send_four(msg_x, i)
+        send_group(msg_x, i)
         return v
 
-    lax.fori_loop(0, wall_count // 4, bwd, jnp.zeros((8, B), F32))
+    lax.fori_loop(0, wall_count // 8, bwd, jnp.zeros((8, B), F32))
     x_in[mine] = x_out[me]
 
     everyone(*msg_x).wait_recv()

time: 74.5 us -> 74.1 us (level)
  no operation moved by 1% of the time
where the time goes in v5:
time: 74.1 us; the launch traced here: 73.9 us
  Pallas kernels  72.5 us (98%)
  local copies, waits for them, and re-layouts  1.47 us (2%)
    pallas_call x1, Pallas kernels, per_device(): pl.pallas_call(kernel, out_shape=jax.ShapeDtypeStruct((2, lines, B), F32)...  72.5 us

profile of v5, /device:TPU:1, one launch (start us, length us, event | category | flops | bytes accessed | tf_op | source)
XLA Modules:
  0.0 73.9 jit_solution(3535499874159062631)
XLA Ops:
  0.0 72.5 %lines.1 = f32[2,32,162]{2,1,0:T(8,128)} custom-call(bf16[64,162]{1,0:T(8,128)(2,1)} %state_hbm.1, bf16[64,162]{1,0:T(8,128)(2,1)} %source_hbm.1, f32[4,64]{1,0:T(4,128)} %bitcast.8, s32[4,64]{1,0:T(4,128)} %bitcast.9, bf16[162,162]{1,0:T(8,128)(2,1)} %lift_hbm.1, s32[2,32]{1,0:T(2,128)} %slot_hbm.1, s32[32]{0:T(128)} %len_ref.1, ...), custom_call_target="tpu_custom_call" | custom-call | tf_op jit(solution)/shard_map/lines/pallas_call | solution.py:450
  72.5 1.5 %copy.12 = f32[2,32,162]{2,1,0:T(8,128)} copy(f32[2,32,162]{2,1,0:T(8,128)} %lines.1) | data formatting | bytes 82944
